TPU v7x, 256 devices: a whole 4x4x8 slice. The times are simulated.
256 devices in a mesh: lat: 4 (over y_hi, core), lon: 64 (over y_lo, z, x).
Axes of the slice: x: 4, y: 4 (y_hi: 2, y_lo: 2; y = y_hi * 2 + y_lo), z: 8, core: 2. Of those that a mesh axis runs over, the one named last changes fastest.
Arguments:
- inputs: bfloat16 [8, 24, 768, 192], P(None, 'lat', 'lon'), may hold values from -6 to 6
- cotangent: bfloat16 [8, 24, 768, 192], P(None, 'lat', 'lon'), may hold values from -6 to 6
- qkv_weight: bfloat16 [192, 576], P(None, 'lon'), may hold values from -0.4375 to 0.4375
- proj_weight: bfloat16 [192, 192], P(None, 'lon'), may hold values from -0.4375 to 0.4375
- up_weight: bfloat16 [192, 768], P(None, 'lon'), may hold values from -0.4375 to 0.4375
- down_weight: bfloat16 [768, 192], P(None, 'lon'), may hold values from -0.21875 to 0.21875
- norm_gains: bfloat16 [2, 192], P(None, 'lon'), may hold values from 0.099609375 to 1.8984375
- bias_table: bfloat16 [16, 6, 20736], P(None, None, 'lon'), may hold values from -4 to 304
- type_of: int32 [4, 4], replicated, may hold values from 0 to 15
- region: int32 [8, 24], P(None, 'lat'), may hold values from 0 to 2
Outputs:
- grad_input: bfloat16 [8, 24, 768, 192], P(None, 'lat', 'lon')
- grad_qkv: float32 [192, 576], P(None, 'lon')
- grad_proj: float32 [192, 192], P(None, 'lon')
- grad_up: float32 [192, 768], P(None, 'lon')
- grad_down: float32 [768, 192], P(None, 'lon')
- grad_gains: float32 [2, 192], P(None, 'lon')
- grad_table: float32 [16, 6, 20736], P(None, None, 'lon')
Inputs may be any that keep to these rules, and one draw needn't show every extreme that they name: `type_of`: types may repeat and some may be absent. Attention joins only tokens of a window with equal region ids.
All inputs are finite; a program needn't handle non-finite values.
Results may differ from a plain program's by a relative error of at most 0.015.
Values may be sent and summed in bfloat16 or wider, within the bound.
No kernel may reach another device: no remote copies, remote signals or barrier semaphores. Data moves between devices by JAX's collectives and lax.ppermute only.
A program may use at most 64 MiB of HBM per device.

v0:
```python
import math

import jax
import jax.numpy as jnp
from jax import lax
from jax.experimental import pallas as pl
from jax.experimental.pallas import tpu as pltpu
from jax.sharding import Mesh, PartitionSpec as P

WPL = 2
WLAT = 6
WLON = 12
WIN = 144
D = 192
HEADS = 6
HEAD = 32
FFN = 768
LON = ("yl", "z", "x")
LAT = ("yh", "core")
F32 = jnp.float32
BF16 = jnp.bfloat16


def passed_along(block, axes, distance):
    size = math.prod(lax.axis_size(a) for a in axes)
    return lax.ppermute(block, axes, [((i - distance) % size, i) for i in range(size)])


def layer_norm(values):
    row_mean = jnp.mean(values, axis=-1, keepdims=True)
    centred = values - row_mean
    variance = jnp.mean(centred * centred, axis=-1, keepdims=True)
    inv_std = lax.rsqrt(variance + 1e-05)
    return (centred * inv_std, inv_std)


def norm_back(d_normed, normed, inv_std):
    return inv_std * (
        d_normed
        - jnp.mean(d_normed, axis=-1, keepdims=True)
        - normed * jnp.mean(d_normed * normed, axis=-1, keepdims=True)
    )


def gelu_pair(pre_act):
    cumul = 0.5 * (1.0 + lax.erf(pre_act * 0.7071067811865476))
    density = jnp.exp(-0.5 * pre_act * pre_act) * 0.3989422804014327
    return (pre_act * cumul, cumul + pre_act * density)


def spread(a, b, contract):
    return lax.dot_general(a, b, ((contract[0], contract[1]), ((), ())), preferred_element_type=F32)


def nt(a, b):
    return spread(a, b, ((1,), (1,)))


def nn(a, b):
    return spread(a, b, ((1,), (0,)))


def tn(a, b):
    return spread(a, b, ((0,), (0,)))


def swap_quarters(rows):
    return jnp.concatenate([rows[:36], rows[72:108], rows[36:72], rows[108:]], axis=0)


def unpack_weights(halves_ref, qkv_ref, proj_ref, up_ref, down_ref):
    def stack(pieces):
        return jnp.concatenate(pieces, axis=0).astype(BF16)

    for g in range(4):
        v = [[halves_ref[c, 16 * g + i].astype(F32) for i in range(16)] for c in range(2)]
        for c in range(2):
            rows = slice(c * 384 + 96 * g, c * 384 + 96 * (g + 1))
            up_ref[rows, :128] = stack([p[:6] for p in v[c]])
            up_ref[rows, 128:] = stack([p[6:9, s : s + 64] for p in v[c] for s in (0, 64)])
            for t in range(3):
                cols = slice(c * 384 + 128 * t, c * 384 + 128 * (t + 1))
                down_ref[48 * g : 48 * (g + 1), cols] = stack(
                    [p[9 + 3 * t : 12 + 3 * t] for p in v[c]]
                )
        rows = slice(144 * g, 144 * (g + 1))
        pairs = list(zip(v[0], v[1]))
        qkv_ref[rows, :128] = stack([q for a, b in pairs for q in (a[18:24], b[18:21])])
        qkv_ref[rows, 128:] = stack(
            [q for a, b in pairs for q in (a[24:27, :64], a[24:27, 64:], b[24:27, :64])]
        )
        rows = slice(48 * g, 48 * (g + 1))
        proj_ref[rows, :128] = stack([b[21:24] for b in v[1]])
        proj_ref[rows, 128:] = stack([b[24:27, 64:] for b in v[1]])


def pack_grads(core, g_qkv, g_proj, g_up, g_down, kept_ref):
    def tails(ref, at, gap):
        return [ref[at : at + 3, 128:], ref[at + gap : at + gap + 3, 128:]]

    for e in range(64):
        for c in range(2):
            at = c * 384 + 6 * e
            ups = [g_up[at : at + 6, :128], jnp.concatenate(tails(g_up, at, 3), axis=1)]
            downs = [
                g_down[3 * e : 3 * e + 3, c * 384 + 128 * t : c * 384 + 128 * (t + 1)]
                for t in range(3)
            ]
            if c == 0:
                rest = [g_qkv[9 * e : 9 * e + 6, :128]]
                ends = tails(g_qkv, 9 * e, 3)
            else:
                rest = [g_qkv[9 * e + 6 : 9 * e + 9, :128], g_proj[3 * e : 3 * e + 3, :128]]
                ends = [g_qkv[9 * e + 6 : 9 * e + 9, 128:], g_proj[3 * e : 3 * e + 3, 128:]]
            rest.append(jnp.concatenate(ends, axis=1))
            piece = jnp.concatenate(ups + downs + rest, axis=0).astype(BF16)
            kept_ref[c if core is None else jnp.where(core == c, 0, 1), e] = piece


def block_kernel(
    last_ref,
    core_ref,
    b0,
    b1,
    b2,
    b3,
    rim_ref,
    halves_ref,
    gains_ref,
    strips_ref,
    row_label_ref,
    col_label_ref,
    back_ref,
    back_rim_ref,
    packed_ref,
    g_gains_ref,
    table_ref,
    qkv_ref,
    proj_ref,
    up_ref,
    down_ref,
    g_qkv,
    g_proj,
    g_up,
    g_down,
    tokens,
    bias_full,
    probs,
    table_sum,
    s_one,
    s_two,
    att_all,
    hid_all,
    dhid_all,
    dmid_all,
    dpack_all,
    d_tokens,
    gain_sums,
):
    factor = 1.0 / math.sqrt(HEAD)
    last = last_ref[0]
    blocks = (b0, b1, b2, b3)
    place = lax.broadcasted_iota(jnp.int32, (WIN, 1), 0) % WLON
    is_left = place < WLON // 2
    same = row_label_ref[...] == col_label_ref[...]
    unpack_weights(halves_ref, qkv_ref, proj_ref, up_ref, down_ref)
    source = lax.broadcasted_iota(jnp.int32, (WIN, 192), 1)
    target = lax.broadcasted_iota(jnp.int32, (WIN, 192), 0)
    held = 9 * (source // 12) + 2 * (source // 3 % 4) + source % 3
    joins = (held == target).astype(F32).astype(BF16)
    for h in range(HEADS):
        bias_full[h] = jnp.where(same, nn(joins, strips_ref[h]), -jnp.inf)
        table_sum[h] = jnp.zeros((WIN, WIN), F32)
    gain_sums[...] = jnp.zeros_like(gain_sums)
    rim = swap_quarters(rim_ref[...].astype(F32))
    natural = [swap_quarters(b[...].astype(F32)) for b in blocks]
    for k in range(4):
        ahead = jnp.where(last == k, rim, natural[k - 1])
        fore = jnp.concatenate([natural[k][6:], natural[k][:6]], axis=0)
        rear = jnp.concatenate([ahead[-6:], ahead[:-6]], axis=0)
        tokens[k] = jnp.where(is_left, fore, rear)
    gain_one = gains_ref[0:1, :].astype(F32)
    gain_two = gains_ref[1:2, :].astype(F32)
    lane = lax.broadcasted_iota(jnp.int32, (1, D), 1) // HEAD
    masks = [(lane == h).astype(BF16) for h in range(HEADS)]

    def one_window(w, carry):
        at = pl.multiple_of(w * WIN, 16)
        rows = pl.ds(at, WIN)
        both = tokens[w]
        cells = both[:, :D]
        cot = both[:, D:]
        cot_b = cot.astype(BF16)
        normed_one, inv_one = layer_norm(cells)
        scaled_one = (normed_one * gain_one).astype(BF16)
        s_one[rows, :] = scaled_one
        queries = nt(scaled_one, qkv_ref[0:D, :]).astype(BF16)
        key_rows = nt(scaled_one, qkv_ref[D : 2 * D, :]).astype(BF16)
        values = nt(scaled_one, qkv_ref[2 * D :, :]).astype(BF16)
        attended = jnp.zeros((WIN, D), F32)
        for h in range(HEADS):
            scores = nt(queries * masks[h], key_rows) * factor + bias_full[h]
            raised = jnp.exp(scores - jnp.max(scores, axis=-1, keepdims=True))
            p = raised * (1.0 / jnp.sum(raised, axis=-1, keepdims=True))
            probs[h] = p
            attended = attended + nn(p.astype(BF16), values * masks[h])
        attended = attended.astype(BF16)
        att_all[rows, :] = attended
        middle = cells + nt(attended, proj_ref[...])
        normed_two, inv_two = layer_norm(middle)
        scaled_two = (normed_two * gain_two).astype(BF16)
        s_two[rows, :] = scaled_two
        d_htwo = jnp.zeros((WIN, D), F32)
        for c in range(3):
            part = slice(c * 256, (c + 1) * 256)
            pre_act = nt(scaled_two, up_ref[part, :])
            activated, slope = gelu_pair(pre_act)
            hid_all[rows, part] = activated.astype(BF16)
            d_hidden = (nn(cot_b, down_ref[:, part]) * slope).astype(BF16)
            dhid_all[rows, part] = d_hidden
            d_htwo = d_htwo + nn(d_hidden, up_ref[part, :])
        gain_sums[1:2, :] += jnp.sum(d_htwo * normed_two, axis=0, keepdims=True)
        d_middle = cot + norm_back(d_htwo * gain_two, normed_two, inv_two)
        d_middle_b = d_middle.astype(BF16)
        dmid_all[rows, :] = d_middle_b
        d_att = nn(d_middle_b, proj_ref[...]).astype(BF16)
        d_queries = jnp.zeros((WIN, D), F32)
        d_keys = jnp.zeros((WIN, D), F32)
        d_values = jnp.zeros((WIN, D), F32)
        for h in range(HEADS):
            p = probs[h]
            d_att_h = d_att * masks[h]
            d_prob = nt(d_att_h, values)
            d_values = d_values + tn(p.astype(BF16), d_att_h)
            d_score = p * (d_prob - jnp.sum(p * d_prob, axis=-1, keepdims=True))
            table_sum[h] += d_score
            d_score_b = d_score.astype(BF16)
            d_queries = d_queries + nn(d_score_b, key_rows * masks[h])
            d_keys = d_keys + tn(d_score_b, queries * masks[h])
        d_q = (d_queries * factor).astype(BF16)
        d_k = (d_keys * factor).astype(BF16)
        d_v = d_values.astype(BF16)
        dpack_all[0, rows, :] = d_q
        dpack_all[1, rows, :] = d_k
        dpack_all[2, rows, :] = d_v
        d_hone = (
            nn(d_q, qkv_ref[0:D, :]) + nn(d_k, qkv_ref[D : 2 * D, :]) + nn(d_v, qkv_ref[2 * D :, :])
        )
        gain_sums[0:1, :] += jnp.sum(d_hone * normed_one, axis=0, keepdims=True)
        d_tokens[w] = d_middle + norm_back(d_hone * gain_one, normed_one, inv_one)
        return carry

    lax.fori_loop(0, 4, one_window, 0)
    for k in range(4):
        mine, following = d_tokens[k], d_tokens[(k + 1) % 4]
        fore = jnp.concatenate([mine[-6:], mine[:-6]], axis=0)
        rear = jnp.concatenate([following[6:], following[:6]], axis=0)
        first = (k + 1) % 4 == last
        back_ref[k] = swap_quarters(
            jnp.where(is_left, jnp.where(first, 0.0, rear), fore)
        ).astype(BF16)

        @pl.when(first)
        def _():
            back_rim_ref[...] = swap_quarters(jnp.where(is_left, rear, 0.0)).astype(BF16)

    for part in range(3):
        g_qkv[part * D : (part + 1) * D, :] = tn(dpack_all[part], s_one[...])
    g_proj[...] = tn(dmid_all[...], att_all[...])
    cots = jnp.concatenate([tokens[k][:, D:] for k in range(4)], axis=0).astype(BF16)
    g_down[...] = tn(cots, hid_all[...])
    g_up[...] = tn(dhid_all[...], s_two[...])
    g_gains_ref[...] = gain_sums[...]
    pack_grads(core_ref[0], g_qkv, g_proj, g_up, g_down, packed_ref)
    for h in range(HEADS):
        table_ref[h] = tn(joins, table_sum[h].astype(BF16)).astype(BF16)


def block_grads(last, core, blocks, rim, halves, gains, strips, row_label, col_label):
    rows = 4 * WIN
    out = [
        ((4, WIN, D), BF16),
        ((WIN, D), BF16),
        ((2, 64, 27, 128), BF16),
        ((2, D), F32),
        ((HEADS, 192, WIN), BF16),
    ]
    scratch = [
        ((3 * D, D), BF16),
        ((D, D), BF16),
        ((FFN, D), BF16),
        ((D, FFN), BF16),
        ((3 * D, D), F32),
        ((D, D), F32),
        ((FFN, D), F32),
        ((D, FFN), F32),
        ((4, WIN, 2 * D), F32),
        ((HEADS, WIN, WIN), F32),
        ((HEADS, WIN, WIN), F32),
        ((HEADS, WIN, WIN), F32),
        ((rows, D), BF16),
        ((rows, D), BF16),
        ((rows, D), BF16),
        ((rows, FFN), BF16),
        ((rows, FFN), BF16),
        ((rows, D), BF16),
        ((3, rows, D), BF16),
        ((4, WIN, D), F32),
        ((2, D), F32),
    ]
    whole = pl.BlockSpec(memory_space=pltpu.VMEM)
    return pl.pallas_call(
        block_kernel,
        in_specs=[pl.BlockSpec(memory_space=pltpu.SMEM)] * 2 + [whole] * 10,
        out_specs=[whole] * len(out),
        out_shape=[jax.ShapeDtypeStruct(s, t) for s, t in out],
        scratch_shapes=[pltpu.VMEM(s, t) for s, t in scratch],
        compiler_params=pltpu.CompilerParams(vmem_limit_bytes=48 << 20),
        name="block_grads",
    )(last.reshape(1), core.reshape(1), *blocks, rim, halves, gains, strips, row_label, col_label)


def shards(
    inputs,
    cotangent,
    qkv_weight,
    proj_weight,
    up_weight,
    down_weight,
    norm_gains,
    bias_table,
    type_of,
    region,
):
    lat_index = lax.axis_index(LAT)
    core = lax.axis_index("core")
    x_index = lax.axis_index("x")
    type_count = bias_table.shape[0]
    positions = type_of.shape[0]
    own = bias_table.shape[2]
    groups = lax.axis_size("yl") * lax.axis_size("z")
    members = lax.axis_size("x")
    lons = groups * members

    cells = jnp.concatenate([inputs, cotangent], axis=-1)
    cells = jnp.roll(cells, -1, axis=0).reshape(positions, WPL, 2, WLAT // 2, WLON, 2 * D)
    cells = cells.transpose(0, 2, 1, 3, 4, 5).reshape(positions, 2, WIN // 2, 2 * D)

    rows = jnp.concatenate([qkv_weight.T, proj_weight.T], axis=0)
    rows = jnp.stack([up_weight.T.reshape(2, 6, D), rows.reshape(2, 6, D)], axis=1)
    ends = rows[..., 128:].reshape(2, 2, 2, 3, 64).transpose(0, 1, 3, 2, 4).reshape(2, 2, 3, 128)
    downs = down_weight.reshape(lons, 2, 6, 3).transpose(1, 3, 0, 2).reshape(2, 3, 3, 128)
    downs = downs.transpose(0, 2, 1, 3).reshape(2, 9, 128)
    both = jnp.concatenate([rows[..., :128], ends], axis=2)
    half = jnp.concatenate([both[:, 0], downs, both[:, 1]], axis=1)
    half = lax.dynamic_index_in_dim(half, core, 0, False)
    types = lax.dynamic_slice(type_of, (jnp.int32(0), lat_index), (positions, 1))[:, 0]
    onehot = types[:, None] == jnp.arange(type_count, dtype=jnp.int32)[None, :]
    slabs = jnp.dot(
        onehot.astype(BF16), bias_table.reshape(type_count, -1), preferred_element_type=F32
    ).astype(BF16)
    slabs = slabs.reshape(positions, HEADS, own)
    slabs = lax.dynamic_update_slice(
        jnp.zeros((positions, HEADS, 3 * WIN), BF16), slabs, (0, 0, x_index * 36)
    ).reshape(positions, -1)
    slab_size = slabs.shape[1]
    gain_part = jnp.broadcast_to(norm_gains.reshape(1, 6), (positions, 6))
    fill = jnp.zeros((positions, 21 * 128 - slab_size - 6), BF16)
    slabs = jnp.concatenate([slabs, gain_part, fill], axis=1).reshape(positions, 21, 128)
    parcel = jnp.concatenate([jnp.broadcast_to(half[None], (positions, 27, 128)), slabs], axis=1)
    parcel = jnp.broadcast_to(parcel[None], (groups, members, 48, 128)).reshape(lons, 48, 128)
    parcel, cells = lax.optimization_barrier((parcel, cells))
    arrived = passed_along(cells[:, 0], LAT, -1)
    landed = lax.all_to_all(parcel, LON, 0, 0)

    halves = lax.all_gather(landed[:, :27], "core", axis=0)
    tail = landed[:, 27:].reshape(lons, 21 * 128)
    gains = tail[:, slab_size : slab_size + 6].reshape(lons, 2, 3).transpose(1, 0, 2).reshape(2, D)
    strips = tail[:, :slab_size].reshape(lons, HEADS, 3, WIN).transpose(1, 0, 2, 3)
    strips = strips.reshape(HEADS, 3 * lons, WIN)

    cells = jnp.concatenate([cells[:, 1], arrived], axis=1)
    cells = jnp.concatenate([cells, cells[: members - 1]], axis=0)
    cells = lax.dynamic_slice_in_dim(cells, x_index, members, 0)
    blocks = [cells[0]] + [passed_along(cells[k], ("x",), k) for k in range(1, members)]
    is_first = [x_index == k for k in range(members)]
    rim = blocks[0]
    for k in range(1, members):
        rim = jnp.where(is_first[k], blocks[k], rim)
    rim = passed_along(rim, ("yl", "z"), -1)
    last = (x_index + 1) % members

    labels = lax.dynamic_slice(region, (x_index * WPL, jnp.int32(0)), (WPL, WLAT))
    labels = jnp.broadcast_to(labels[:, :, None], (WPL, WLAT, WLON)).reshape(WIN)
    back, rim, packed, g_gains, strips = block_grads(
        last, core, blocks, rim, halves, gains, strips, labels.reshape(WIN, 1), labels.reshape(1, WIN)
    )

    g_half = packed[0].astype(F32) + passed_along(packed[1], ("core",), 1).astype(F32)
    g_half = g_half.astype(BF16)
    strips = strips.reshape(HEADS, lons, 3, WIN).transpose(1, 0, 2, 3).reshape(lons, slab_size)
    g_gain_part = g_gains.reshape(2, lons, 3).transpose(1, 0, 2).reshape(lons, 6).astype(BF16)
    fill = jnp.zeros((lons, 21 * 128 - slab_size - 6), BF16)
    strips = jnp.concatenate([strips, g_gain_part, fill], axis=1).reshape(lons, 21, 128)
    parcel = jnp.concatenate([g_half, strips], axis=1)
    parcel, rim = lax.optimization_barrier((parcel, rim))
    returned = lax.all_to_all(parcel, LON, 0, 0)
    rim = passed_along(rim, ("yl", "z"), 1)
    blocks = [jnp.where(is_first[k], back[k] + rim, back[k]) for k in range(members)]
    blocks = [blocks[0]] + [passed_along(blocks[k], ("x",), -k) for k in range(1, members)]
    back = jnp.stack(blocks + blocks[: members - 1])
    back = lax.dynamic_slice_in_dim(back, (members - x_index) % members, members, 0)
    back = back.reshape(positions, 2, WIN // 2, D)
    arrived = passed_along(back[:, 1], LAT, 1)
    back = jnp.stack([arrived, back[:, 0]], axis=1)
    back = back.reshape(positions, 2, WPL, WLAT // 2, WLON, D).transpose(0, 2, 1, 3, 4, 5)
    grad_input = jnp.roll(back.reshape(inputs.shape), 1, axis=0)

    returned = returned.astype(F32)
    half_sum = jnp.sum(returned[:, :27], axis=0).reshape(-1)
    half_size = half_sum.shape[0]
    strip_sum = jnp.sum(returned[:, 27:].reshape(groups, members, 21 * 128), axis=0)
    table_part = lax.dynamic_slice(
        strip_sum[:, :slab_size].reshape(positions, HEADS, 3 * WIN),
        (jnp.int32(0), jnp.int32(0), x_index * 36),
        (positions, HEADS, own),
    )
    gain_sum = jnp.sum(strip_sum[:, slab_size : slab_size + 6], axis=0)
    note = jnp.concatenate([half_sum, table_part.reshape(-1), gain_sum])
    size = note.shape[0]
    note = jnp.pad(note.astype(BF16), (0, -size % 1024)).reshape(-1, 128)
    notes = lax.all_gather(note, LAT, axis=0).astype(F32).reshape(4, -1)
    whole = jnp.sum(notes[:, :half_size].reshape(2, 2, 27, 128), axis=0)
    table_size = positions * HEADS * own
    terms = notes[:, half_size : half_size + table_size].reshape(4 * positions, -1)
    gain_total = jnp.sum(notes[:, half_size + table_size : size], axis=0).reshape(2, 3)
    all_types = type_of.T.reshape(-1)
    select = jnp.arange(type_count, dtype=jnp.int32)[:, None] == all_types[None, :]
    grad_table = jnp.dot(select.astype(F32), terms, precision=lax.Precision.HIGHEST)
    factor = 1.0 / math.sqrt(inputs.shape[0] * inputs.shape[1] * inputs.shape[2] * 4 * lons)
    whole = whole * factor

    def joined(at):
        ends = whole[:, at + 6 : at + 9].reshape(2, 3, 2, 64).transpose(0, 2, 1, 3)
        rows = jnp.concatenate([whole[:, at : at + 6], ends.reshape(2, 6, 64)], axis=2)
        return rows.reshape(12, D)

    grad_up = joined(0).T
    rows = joined(18)
    grad_qkv = rows[:9].T
    grad_proj = rows[9:].T
    grad_down = whole[:, 9:18].reshape(2, 3, 3, 128).transpose(0, 2, 1, 3).reshape(2, 3, lons, 6)
    grad_down = grad_down.transpose(2, 0, 3, 1).reshape(FFN, 3)
    return (
        grad_input,
        grad_qkv,
        grad_proj,
        grad_up,
        grad_down,
        gain_total * factor,
        grad_table.reshape(type_count, HEADS, own),
    )


def solution(mesh):
    finer = Mesh(mesh.devices.reshape(2, 2, 2, 8, 4), ("yh", "core", "yl", "z", "x"))
    return jax.shard_map(
        shards,
        mesh=finer,
        in_specs=(
            P(None, LAT, LON, None),
            P(None, LAT, LON, None),
            P(None, LON),
            P(None, LON),
            P(None, LON),
            P(None, LON),
            P(None, LON),
            P(None, None, LON),
            P(),
            P(None, LAT),
        ),
        out_specs=(
            P(None, LAT, LON, None),
            P(None, LON),
            P(None, LON),
            P(None, LON),
            P(None, LON),
            P(None, LON),
            P(None, None, LON),
        ),
        check_vma=False,
    )
```

profile of v0, /device:TPU:1, one launch (start us, length us, event | category | flops | bytes accessed | tf_op | source)
XLA Modules:
  0.0 131.4 jit_solution(14172647704034759037)
XLA Ops:
  2.2 0.9 copy.112
  3.3 0.9 fusion.17
  5.8 0.9 reshape.161
  6.9 1.3 slice_maximum_fusion
  9.2 1.0 broadcast_in_dim.44
  10.2 14.1 %all-to-all-start = ((bf16[64,48,128]{2,1,0:T(8,128)(2,1)}), bf16[64,48,128]{2,1,0:T(8,128)(2,1)S(1)}, u32[]{:S(2)}, u32[]{:S(2)}) async-start(bf16[64,48,128]{2,1,0:T(8,128)(2,1)} %bitcast.13), calls=%async_computation | async-start | bytes 1572864 | tf_op jit(solution)/shard_map/all_to_all | solution.py:374
  24.4 1.0 collective-permute-start
  25.4 8.3 %collective-permute-done = bf16[4,72,384]{2,1,0:T(8,128)(2,1)S(1)} collective-permute-done((bf16[4,72,384]{2,1,0:T(8,128)(2,1)S(1)}, bf16[4,72,384]{2,1,0:T(8,128)(2,1)S(1)}, u32[]{:S(2)}, u32[]{:S(2)}) %collective-permute-start) | collective-permute-done | bytes 221216 | tf_op jit(solution)/shard_map/ppermute | solution.py:26
  34.4 2.0 %collective-permute-start.1 = (bf16[144,384]{1,0:T(8,128)(2,1)S(1)}, bf16[144,384]{1,0:T(8,128)(2,1)S(1)}, u32[]{:S(2)}, u32[]{:S(2)}) collective-permute-start(bf16[144,384]{1,0:T(8,128)(2,1)S(1)} %get-tuple-element.27), channel_id=1, source_target_pairs={{3,0},{0,1},{1,2},{2,3},{7,4},{4,5},{5,6},{6,7},{11,8},{8,9},{9,10... | collective-permute-start | bytes 331784 | tf_op jit(solution)/shard_map/ppermute | solution.py:26
  36.4 2.0 %collective-permute-start.2 = (bf16[144,384]{1,0:T(8,128)(2,1)S(1)}, bf16[144,384]{1,0:T(8,128)(2,1)S(1)}, u32[]{:S(2)}, u32[]{:S(2)}) collective-permute-start(bf16[144,384]{1,0:T(8,128)(2,1)S(1)} %get-tuple-element.26), channel_id=1, source_target_pairs={{2,0},{3,1},{0,2},{1,3},{6,4},{7,5},{4,6},{5,7},{10,8},{11,9},{8,1... | collective-permute-start | bytes 331784 | tf_op jit(solution)/shard_map/ppermute | solution.py:26
  38.5 1.5 %collective-permute-start.3 = (bf16[144,384]{1,0:T(8,128)(2,1)S(1)}, bf16[144,384]{1,0:T(8,128)(2,1)S(1)}, u32[]{:S(2)}, u32[]{:S(2)}) collective-permute-start(bf16[144,384]{1,0:T(8,128)(2,1)S(1)} %get-tuple-element.25), channel_id=1, source_target_pairs={{1,0},{2,1},{3,2},{0,3},{5,4},{6,5},{7,6},{4,7},{9,8},{10,9},{11,1... | collective-permute-start | bytes 331784 | tf_op jit(solution)/shard_map/ppermute | solution.py:26
  40.2 3.7 %collective-permute-done.1.b1 = bf16[144,384]{1,0:T(8,128)(2,1)S(1)} collective-permute-done((bf16[144,384]{1,0:T(8,128)(2,1)S(1)}, bf16[144,384]{1,0:T(8,128)(2,1)S(1)}, u32[]{:S(2)}, u32[]{:S(2)}) %collective-permute-start.1) | collective-permute-done | bytes 110624 | tf_op jit(solution)/shard_map/ppermute | solution.py:26
  43.9 2.7 %collective-permute-done.2.b2 = bf16[144,384]{1,0:T(8,128)(2,1)S(1)} collective-permute-done((bf16[144,384]{1,0:T(8,128)(2,1)S(1)}, bf16[144,384]{1,0:T(8,128)(2,1)S(1)}, u32[]{:S(2)}, u32[]{:S(2)}) %collective-permute-start.2) | collective-permute-done | bytes 110624 | tf_op jit(solution)/shard_map/ppermute | solution.py:26
  46.7 3.2 %collective-permute-start.4 = (bf16[144,384]{1,0:T(8,128)(2,1)S(1)}, bf16[144,384]{1,0:T(8,128)(2,1)S(1)}, u32[]{:S(2)}, u32[]{:S(2)}) collective-permute-start(bf16[144,384]{1,0:T(8,128)(2,1)S(1)} %select_select_fusion), channel_id=1, source_target_pairs={{4,0},{8,4},{12,8},{16,12},{20,16},{24,20},{28,24},{32,28},{36,32}... | collective-permute-start | bytes 331784 | tf_op jit(solution)/shard_map/ppermute | solution.py:26
  50.1 2.9 %all-gather = bf16[128,27,128]{2,0,1:T(8,128)(2,1)S(1)} all-gather(bf16[64,27,128]{2,0,1:T(8,128)(2,1)S(1)} %copy.116), channel_id=2, replica_groups=mesh['yh'=2,'core'=2,'yl'=2,'z'=8,'x'=4] {'core'}, dimensions={0}, use_global_device_ids=true | all-gather | bytes 1327104 | tf_op jit(solution)/shard_map/all_gather | solution.py:376
  53.2 0.9 reshape.174
  55.9 20.2 %block_grads.1 = (bf16[4,144,192]{2,1,0:T(8,128)(2,1)S(1)}, bf16[144,192]{1,0:T(8,128)(2,1)S(1)}, bf16[2,64,27,128]{3,2,1,0:T(8,128)(2,1)S(1)}, f32[2,192]{1,0:T(2,128)S(1)}, bf16[6,192,144]{2,1,0:T(8,128)(2,1)S(1)}) custom-call(s32[1]{0:T(128)} %bitcast.last_ref, s32[1]{0:T(128)} %bitcast.1.core_ref, bf16[144,384]{1,0:T(8,128)(2,1)S(1)} %get-tuple-element.28.b0, ...), custom_call_target="tpu_custom_call" | custom-call | tf_op jit(solution)/shard_map/block_grads/pallas_call | solution.py:312
  76.1 0.8 slice_bitcast_fusion
  77.4 1.1 reshape.176
  78.4 2.3 %copy.122 = bf16[64,6,3,144]{3,2,1,0:T(4,128)(2,1)} copy(bf16[64,6,3,144]{3,2,0,1:T(4,128)(2,1)} %bitcast.138) | data formatting | bytes 663552 | tf_op jit(solution)/shard_map/transpose | solution.py:401
  80.7 1.8 %reshape.177 = bf16[64,2592]{1,0:T(8,128)(2,1)S(1)} reshape(bf16[64,6,3,144]{3,2,1,0:T(4,128)(2,1)} %copy.122) | data formatting | bytes 663552 | tf_op jit(solution)/shard_map/reshape | solution.py:401
  83.3 1.2 fusion
  84.5 1.1 pad_maximum_fusion
  85.6 8.6 %all-to-all-start.1 = ((bf16[64,48,128]{2,1,0:T(8,128)(2,1)}), bf16[64,48,128]{2,1,0:T(8,128)(2,1)S(1)}, u32[]{:S(2)}, u32[]{:S(2)}) async-start(bf16[64,48,128]{2,1,0:T(8,128)(2,1)} %pad_maximum_fusion), calls=%async_computation.1 | async-start | bytes 1572864 | tf_op jit(solution)/shard_map/all_to_all | solution.py:407
  94.2 2.3 %collective-permute-start.7 = (bf16[144,192]{1,0:T(8,128)(2,1)S(1)}, bf16[144,192]{1,0:T(8,128)(2,1)S(1)}, u32[]{:S(2)}, u32[]{:S(2)}) collective-permute-start(bf16[144,192]{1,0:T(8,128)(2,1)S(1)} %get-tuple-element.33), channel_id=1, source_target_pairs={{1,0},{2,1},{3,2},{0,3},{5,4},{6,5},{7,6},{4,7},{9,8},{10,9},{11,1... | collective-permute-start | bytes 165896 | tf_op jit(solution)/shard_map/ppermute | solution.py:26
  98.4 3.5 %collective-permute-done.8 = bf16[144,192]{1,0:T(8,128)(2,1)S(1)} collective-permute-done((bf16[144,192]{1,0:T(8,128)(2,1)S(1)}, bf16[144,192]{1,0:T(8,128)(2,1)S(1)}, u32[]{:S(2)}, u32[]{:S(2)}) %collective-permute-start.8) | collective-permute-done | bytes 55328 | tf_op jit(solution)/shard_map/ppermute | solution.py:26
  101.9 2.6 %collective-permute-done.9 = bf16[144,192]{1,0:T(8,128)(2,1)S(1)} collective-permute-done((bf16[144,192]{1,0:T(8,128)(2,1)S(1)}, bf16[144,192]{1,0:T(8,128)(2,1)S(1)}, u32[]{:S(2)}, u32[]{:S(2)}) %collective-permute-start.9) | collective-permute-done | bytes 55328 | tf_op jit(solution)/shard_map/ppermute | solution.py:26
  104.6 4.6 %collective-permute-start.10 = (bf16[4,72,192]{2,1,0:T(8,128)(2,1)S(1)}, bf16[4,72,192]{2,1,0:T(8,128)(2,1)S(1)}, u32[]{:S(2)}, u32[]{:S(2)}) collective-permute-start(bf16[4,72,192]{2,1,0:T(8,128)(2,1)S(1)} %get-tuple-element.34), channel_id=1, source_target_pairs={{192,0},{0,64},{64,128},{128,192},{193,1},{1,65},{65,129},{129,193... | collective-permute-start | bytes 331784 | tf_op jit(solution)/shard_map/ppermute | solution.py:26
  109.5 3.5 %collective-permute-done.10 = bf16[4,72,192]{2,1,0:T(8,128)(2,1)S(1)} collective-permute-done((bf16[4,72,192]{2,1,0:T(8,128)(2,1)S(1)}, bf16[4,72,192]{2,1,0:T(8,128)(2,1)S(1)}, u32[]{:S(2)}, u32[]{:S(2)}) %collective-permute-start.10) | collective-permute-done | bytes 110624 | tf_op jit(solution)/shard_map/ppermute | solution.py:26
  113.9 0.9 pad_maximum_fusion.2
  116.8 9.2 %all_gather.11 = bf16[4,88,128]{2,1,0:T(8,128)(2,1)S(1)} all-gather(bf16[1,88,128]{2,1,0:T(8,128)(2,1)S(1)} %pad_bitcast_fusion), channel_id=1, replica_groups=mesh['yh'=2,'core'=2,'yl'=2,'z'=8,'x'=4] {'yh','core'}, dimensions={0}, use_global_device_ids=true | all-gather | bytes 112640 | tf_op jit(solution)/shard_map/all_gather | solution.py:432
  128.0 0.9 reshape.192
  (144 shorter events, 18.3 us)
Async XLA Ops:
  0.6 39.3 %copy-start = (s32[8,6]{1,0:T(8,128)S(1)}, s32[8,6]{1,0:T(8,128)}, u32[]{:S(2)}) copy-start(s32[8,6]{1,0:T(8,128)} %param.19) | copy-start | bytes 580
  0.6 7.6 %copy-start.2 = (bf16[8,6,12,192]{3,0,2,1:T(8,128)(2,1)S(1)}, bf16[8,6,12,192]{3,0,2,1:T(8,128)(2,1)}, u32[]{:S(2)}) copy-start(bf16[8,6,12,192]{3,0,2,1:T(8,128)(2,1)} %param.10) | copy-start | bytes 663556
  0.7 7.6 %copy-start.1 = (bf16[8,6,12,192]{3,0,2,1:T(8,128)(2,1)S(1)}, bf16[8,6,12,192]{3,0,2,1:T(8,128)(2,1)}, u32[]{:S(2)}) copy-start(bf16[8,6,12,192]{3,0,2,1:T(8,128)(2,1)} %param.11) | copy-start | bytes 663556
  10.2 39.6 %all-to-all-start = ((bf16[64,48,128]{2,1,0:T(8,128)(2,1)}), bf16[64,48,128]{2,1,0:T(8,128)(2,1)S(1)}, u32[]{:S(2)}, u32[]{:S(2)}) async-start(bf16[64,48,128]{2,1,0:T(8,128)(2,1)} %bitcast.13), calls=%async_computation | async-start | bytes 1572864 | tf_op jit(solution)/shard_map/all_to_all | solution.py:374
  24.4 9.3 %collective-permute-start = (bf16[4,72,384]{2,1,0:T(8,128)(2,1)S(1)}, bf16[4,72,384]{2,1,0:T(8,128)(2,1)S(1)}, u32[]{:S(2)}, u32[]{:S(2)}) collective-permute-start(bf16[4,72,384]{2,1,0:T(8,128)(2,1)S(1)} %get-tuple-element.29), channel_id=1, source_target_pairs={{64,0},{128,64},{192,128},{0,192},{65,1},{129,65},{193,129},{1,193... | collective-permute-start | bytes 663560 | tf_op jit(solution)/shard_map/ppermute | solution.py:26
  34.4 9.5 %collective-permute-start.1 = (bf16[144,384]{1,0:T(8,128)(2,1)S(1)}, bf16[144,384]{1,0:T(8,128)(2,1)S(1)}, u32[]{:S(2)}, u32[]{:S(2)}) collective-permute-start(bf16[144,384]{1,0:T(8,128)(2,1)S(1)} %get-tuple-element.27), channel_id=1, source_target_pairs={{3,0},{0,1},{1,2},{2,3},{7,4},{4,5},{5,6},{6,7},{11,8},{8,9},{9,10... | collective-permute-start | bytes 331784 | tf_op jit(solution)/shard_map/ppermute | solution.py:26
  36.4 10.2 %collective-permute-start.2 = (bf16[144,384]{1,0:T(8,128)(2,1)S(1)}, bf16[144,384]{1,0:T(8,128)(2,1)S(1)}, u32[]{:S(2)}, u32[]{:S(2)}) collective-permute-start(bf16[144,384]{1,0:T(8,128)(2,1)S(1)} %get-tuple-element.26), channel_id=1, source_target_pairs={{2,0},{3,1},{0,2},{1,3},{6,4},{7,5},{4,6},{5,7},{10,8},{11,9},{8,1... | collective-permute-start | bytes 331784 | tf_op jit(solution)/shard_map/ppermute | solution.py:26
  38.5 8.2 %collective-permute-start.3 = (bf16[144,384]{1,0:T(8,128)(2,1)S(1)}, bf16[144,384]{1,0:T(8,128)(2,1)S(1)}, u32[]{:S(2)}, u32[]{:S(2)}) collective-permute-start(bf16[144,384]{1,0:T(8,128)(2,1)S(1)} %get-tuple-element.25), channel_id=1, source_target_pairs={{1,0},{2,1},{3,2},{0,3},{5,4},{6,5},{7,6},{4,7},{9,8},{10,9},{11,1... | collective-permute-start | bytes 331784 | tf_op jit(solution)/shard_map/ppermute | solution.py:26
  46.7 9.3 %collective-permute-start.4 = (bf16[144,384]{1,0:T(8,128)(2,1)S(1)}, bf16[144,384]{1,0:T(8,128)(2,1)S(1)}, u32[]{:S(2)}, u32[]{:S(2)}) collective-permute-start(bf16[144,384]{1,0:T(8,128)(2,1)S(1)} %select_select_fusion), channel_id=1, source_target_pairs={{4,0},{8,4},{12,8},{16,12},{20,16},{24,20},{28,24},{32,28},{36,32}... | collective-permute-start | bytes 331784 | tf_op jit(solution)/shard_map/ppermute | solution.py:26
  77.0 6.3 %collective-permute-start.5 = (bf16[64,27,128]{2,1,0:T(8,128)(2,1)}, bf16[64,27,128]{2,1,0:T(8,128)(2,1)}, u32[]{:S(2)}, u32[]{:S(2)}) collective-permute-start(bf16[64,27,128]{2,1,0:T(8,128)(2,1)} %slice_bitcast_fusion), channel_id=1, source_target_pairs={{64,0},{0,64},{65,1},{1,65},{66,2},{2,66},{67,3},{3,67},{68,4},{4,... | collective-permute-start | bytes 1327112 | tf_op jit(solution)/shard_map/ppermute | solution.py:26
  85.6 8.6 %collective-permute-start.6 = (bf16[144,192]{1,0:T(8,128)(2,1)S(1)}, bf16[144,192]{1,0:T(8,128)(2,1)S(1)}, u32[]{:S(2)}, u32[]{:S(2)}) collective-permute-start(bf16[144,192]{1,0:T(8,128)(2,1)S(1)} %get-tuple-element.23), channel_id=1, source_target_pairs={{60,0},{0,4},{4,8},{8,12},{12,16},{16,20},{20,24},{24,28},{28,32},... | collective-permute-start | bytes 165896 | tf_op jit(solution)/shard_map/ppermute | solution.py:26
  85.6 30.0 %all-to-all-start.1 = ((bf16[64,48,128]{2,1,0:T(8,128)(2,1)}), bf16[64,48,128]{2,1,0:T(8,128)(2,1)S(1)}, u32[]{:S(2)}, u32[]{:S(2)}) async-start(bf16[64,48,128]{2,1,0:T(8,128)(2,1)} %pad_maximum_fusion), calls=%async_computation.1 | async-start | bytes 1572864 | tf_op jit(solution)/shard_map/all_to_all | solution.py:407
  94.2 15.1 %copy-start.3 = (s32[4,4]{1,0:T(4,128)S(1)}, s32[4,4]{1,0:T(4,128)}, u32[]{:S(2)}) copy-start(s32[4,4]{1,0:T(4,128)} %param.18) | copy-start | bytes 196
  94.2 4.2 %collective-permute-start.7 = (bf16[144,192]{1,0:T(8,128)(2,1)S(1)}, bf16[144,192]{1,0:T(8,128)(2,1)S(1)}, u32[]{:S(2)}, u32[]{:S(2)}) collective-permute-start(bf16[144,192]{1,0:T(8,128)(2,1)S(1)} %get-tuple-element.33), channel_id=1, source_target_pairs={{1,0},{2,1},{3,2},{0,3},{5,4},{6,5},{7,6},{4,7},{9,8},{10,9},{11,1... | collective-permute-start | bytes 165896 | tf_op jit(solution)/shard_map/ppermute | solution.py:26
  96.5 5.4 %collective-permute-start.8 = (bf16[144,192]{1,0:T(8,128)(2,1)S(1)}, bf16[144,192]{1,0:T(8,128)(2,1)S(1)}, u32[]{:S(2)}, u32[]{:S(2)}) collective-permute-start(bf16[144,192]{1,0:T(8,128)(2,1)S(1)} %get-tuple-element.32), channel_id=1, source_target_pairs={{2,0},{3,1},{0,2},{1,3},{6,4},{7,5},{4,6},{5,7},{10,8},{11,9},{8,1... | collective-permute-start | bytes 165896 | tf_op jit(solution)/shard_map/ppermute | solution.py:26
  97.1 7.4 %collective-permute-start.9 = (bf16[144,192]{1,0:T(8,128)(2,1)S(1)}, bf16[144,192]{1,0:T(8,128)(2,1)S(1)}, u32[]{:S(2)}, u32[]{:S(2)}) collective-permute-start(bf16[144,192]{1,0:T(8,128)(2,1)S(1)} %get-tuple-element.31), channel_id=1, source_target_pairs={{3,0},{0,1},{1,2},{2,3},{7,4},{4,5},{5,6},{6,7},{11,8},{8,9},{9,10... | collective-permute-start | bytes 165896 | tf_op jit(solution)/shard_map/ppermute | solution.py:26
  104.6 8.3 %collective-permute-start.10 = (bf16[4,72,192]{2,1,0:T(8,128)(2,1)S(1)}, bf16[4,72,192]{2,1,0:T(8,128)(2,1)S(1)}, u32[]{:S(2)}, u32[]{:S(2)}) collective-permute-start(bf16[4,72,192]{2,1,0:T(8,128)(2,1)S(1)} %get-tuple-element.34), channel_id=1, source_target_pairs={{192,0},{0,64},{64,128},{128,192},{193,1},{1,65},{65,129},{129,193... | collective-permute-start | bytes 331784 | tf_op jit(solution)/shard_map/ppermute | solution.py:26
where the time goes:
time: 132 us; the launch traced here: 131 us
  starting transfers between devices  40.8 us (31%)
  waiting for transfers between devices  25.8 us (20%)
  local copies, waits for them, and re-layouts  22.4 us (17%)
  Pallas kernels  20.2 us (15%)
  blocking collectives  12.1 us (9%)
  other arithmetic  7.67 us (6%)
  between operations  1.32 us (1%)
    ppermute x11, waiting for transfers between devices, passed_along(): lax.ppermute(block, axes, [((i - distance) % size, i) for i in range(size)])  25 us
    pallas_call x1, Pallas kernels, block_grads(): pl.pallas_call(block_kernel, in_specs=[pl.BlockSpec(memory_space=pltpu.SM...  20.2 us
    ppermute x11, starting transfers between devices, passed_along(): lax.ppermute(block, axes, [((i - distance) % size, i) for i in range(size)])  18.2 us
    all_to_all x1, starting transfers between devices, shards(): landed = lax.all_to_all(parcel, LON, 0, 0)  14.1 us
    all_gather x1, blocking collectives, shards(): notes = lax.all_gather(note, LAT, axis=0).astype(F32).reshape(4, -1)  9.24 us
    all_to_all x1, starting transfers between devices, shards(): returned = lax.all_to_all(parcel, LON, 0, 0)  8.59 us
    all_gather x1, blocking collectives, shards(): halves = lax.all_gather(landed[:, :27], 'core', axis=0)  2.9 us
    reshape x2, local copies, waits for them, and re-layouts, shards(): strips.reshape(HEADS, lons, 3, WIN).transpose(1, 0, 2, 3)  2.84 us
  transfers between devices with their start and end apart: 13, of which 8 were waited for; matrix products, arithmetic and copies ran while one was open for 9% of the time, Pallas kernels for 0%

commit v1 on v0

--- a/solution.py
+++ b/solution.py
@@ -94,11 +94,12 @@
         proj_ref[rows, 128:] = stack([b[24:27, 64:] for b in v[1]])
 
 
-def pack_grads(core, g_qkv, g_proj, g_up, g_down, kept_ref):
+def pack_grads(core, g_qkv, g_proj, g_up, g_down, kept_ref, given_ref):
     def tails(ref, at, gap):
         return [ref[at : at + 3, 128:], ref[at + gap : at + gap + 3, 128:]]
 
     for e in range(64):
+        pieces = []
         for c in range(2):
             at = c * 384 + 6 * e
             ups = [g_up[at : at + 6, :128], jnp.concatenate(tails(g_up, at, 3), axis=1)]
@@ -113,8 +114,9 @@
                 rest = [g_qkv[9 * e + 6 : 9 * e + 9, :128], g_proj[3 * e : 3 * e + 3, :128]]
                 ends = [g_qkv[9 * e + 6 : 9 * e + 9, 128:], g_proj[3 * e : 3 * e + 3, 128:]]
             rest.append(jnp.concatenate(ends, axis=1))
-            piece = jnp.concatenate(ups + downs + rest, axis=0).astype(BF16)
-            kept_ref[c if core is None else jnp.where(core == c, 0, 1), e] = piece
+            pieces.append(jnp.concatenate(ups + downs + rest, axis=0))
+        kept_ref[e] = jnp.where(core == 0, pieces[0], pieces[1]).astype(BF16)
+        given_ref[e] = jnp.where(core == 0, pieces[1], pieces[0]).astype(BF16)
 
 
 def block_kernel(
@@ -126,15 +128,14 @@
     b3,
     rim_ref,
     halves_ref,
-    gains_ref,
-    strips_ref,
+    landed_ref,
     row_label_ref,
     col_label_ref,
     back_ref,
     back_rim_ref,
-    packed_ref,
-    g_gains_ref,
-    table_ref,
+    kept_ref,
+    given_ref,
+    strips_ref,
     qkv_ref,
     proj_ref,
     up_ref,
@@ -146,6 +147,11 @@
     tokens,
     bias_full,
     probs,
+    d_probs,
+    probs_b,
+    scores_b,
+    heads_q,
+    heads_d,
     table_sum,
     s_one,
     s_two,
@@ -168,9 +174,18 @@
     target = lax.broadcasted_iota(jnp.int32, (WIN, 192), 0)
     held = 9 * (source // 12) + 2 * (source // 3 % 4) + source % 3
     joins = (held == target).astype(F32).astype(BF16)
+    strips = [landed_ref[e, 24:48, :].astype(F32)[3:] for e in range(64)]
+    ends = jnp.concatenate([p[18:] for p in strips], axis=0).astype(BF16)
+    bias_ends = nn(joins, ends)
     for h in range(HEADS):
-        bias_full[h] = jnp.where(same, nn(joins, strips_ref[h]), -jnp.inf)
+        main = jnp.concatenate([p[3 * h : 3 * h + 3] for p in strips], axis=0).astype(BF16)
+        row = jnp.concatenate([nn(joins, main), bias_ends[:, 16 * h : 16 * h + 16]], axis=1)
+        bias_full[h] = jnp.where(same, row, -jnp.inf)
         table_sum[h] = jnp.zeros((WIN, WIN), F32)
+    gain_lane = lax.broadcasted_iota(jnp.int32, (8, 128), 1) - 96
+    gain_lane = gain_lane == lax.broadcasted_iota(jnp.int32, (8, 128), 0)
+    gain_lane = gain_lane.astype(F32).astype(BF16)
+    gains = nt(gain_lane, ends)
     gain_sums[...] = jnp.zeros_like(gain_sums)
     rim = swap_quarters(rim_ref[...].astype(F32))
     natural = [swap_quarters(b[...].astype(F32)) for b in blocks]
@@ -179,10 +194,17 @@
         fore = jnp.concatenate([natural[k][6:], natural[k][:6]], axis=0)
         rear = jnp.concatenate([ahead[-6:], ahead[:-6]], axis=0)
         tokens[k] = jnp.where(is_left, fore, rear)
-    gain_one = gains_ref[0:1, :].astype(F32)
-    gain_two = gains_ref[1:2, :].astype(F32)
+    gain_one = gains[0:1, :]
+    gain_two = gains[1:2, :]
     lane = lax.broadcasted_iota(jnp.int32, (1, D), 1) // HEAD
     masks = [(lane == h).astype(BF16) for h in range(HEADS)]
+    of_head = [slice(h * WIN, (h + 1) * WIN) for h in range(HEADS)]
+
+    def own_lanes(stacked):
+        out = stacked[of_head[0]]
+        for h in range(1, HEADS):
+            out = jnp.where(lane == h, stacked[of_head[h]], out)
+        return out
 
     def one_window(w, carry):
         at = pl.multiple_of(w * WIN, 16)
@@ -197,13 +219,16 @@
         queries = nt(scaled_one, qkv_ref[0:D, :]).astype(BF16)
         key_rows = nt(scaled_one, qkv_ref[D : 2 * D, :]).astype(BF16)
         values = nt(scaled_one, qkv_ref[2 * D :, :]).astype(BF16)
-        attended = jnp.zeros((WIN, D), F32)
         for h in range(HEADS):
-            scores = nt(queries * masks[h], key_rows) * factor + bias_full[h]
+            heads_q[of_head[h], :] = queries * masks[h]
+        probs[...] = nt(heads_q[...], key_rows)
+        for h in range(HEADS):
+            scores = probs[of_head[h], :] * factor + bias_full[h]
             raised = jnp.exp(scores - jnp.max(scores, axis=-1, keepdims=True))
             p = raised * (1.0 / jnp.sum(raised, axis=-1, keepdims=True))
-            probs[h] = p
-            attended = attended + nn(p.astype(BF16), values * masks[h])
+            probs[of_head[h], :] = p
+            probs_b[of_head[h], :] = p.astype(BF16)
+        attended = own_lanes(nn(probs_b[...], values))
         attended = attended.astype(BF16)
         att_all[rows, :] = attended
         middle = cells + nt(attended, proj_ref[...])
@@ -224,19 +249,18 @@
         d_middle_b = d_middle.astype(BF16)
         dmid_all[rows, :] = d_middle_b
         d_att = nn(d_middle_b, proj_ref[...]).astype(BF16)
-        d_queries = jnp.zeros((WIN, D), F32)
-        d_keys = jnp.zeros((WIN, D), F32)
-        d_values = jnp.zeros((WIN, D), F32)
         for h in range(HEADS):
-            p = probs[h]
-            d_att_h = d_att * masks[h]
-            d_prob = nt(d_att_h, values)
-            d_values = d_values + tn(p.astype(BF16), d_att_h)
+            heads_d[of_head[h], :] = d_att * masks[h]
+        d_probs[...] = nt(heads_d[...], values)
+        for h in range(HEADS):
+            p = probs[of_head[h], :]
+            d_prob = d_probs[of_head[h], :]
             d_score = p * (d_prob - jnp.sum(p * d_prob, axis=-1, keepdims=True))
             table_sum[h] += d_score
-            d_score_b = d_score.astype(BF16)
-            d_queries = d_queries + nn(d_score_b, key_rows * masks[h])
-            d_keys = d_keys + tn(d_score_b, queries * masks[h])
+            scores_b[of_head[h], :] = d_score.astype(BF16)
+        d_queries = own_lanes(nn(scores_b[...], key_rows))
+        d_keys = tn(scores_b[...], heads_q[...])
+        d_values = tn(probs_b[...], heads_d[...])
         d_q = (d_queries * factor).astype(BF16)
         d_k = (d_keys * factor).astype(BF16)
         d_v = d_values.astype(BF16)
@@ -250,7 +274,7 @@
         d_tokens[w] = d_middle + norm_back(d_hone * gain_one, normed_one, inv_one)
         return carry
 
-    lax.fori_loop(0, 4, one_window, 0)
+    lax.fori_loop(0, 4, one_window, 0, unroll=4)
     for k in range(4):
         mine, following = d_tokens[k], d_tokens[(k + 1) % 4]
         fore = jnp.concatenate([mine[-6:], mine[:-6]], axis=0)
@@ -270,20 +294,24 @@
     cots = jnp.concatenate([tokens[k][:, D:] for k in range(4)], axis=0).astype(BF16)
     g_down[...] = tn(cots, hid_all[...])
     g_up[...] = tn(dhid_all[...], s_two[...])
-    g_gains_ref[...] = gain_sums[...]
-    pack_grads(core_ref[0], g_qkv, g_proj, g_up, g_down, packed_ref)
-    for h in range(HEADS):
-        table_ref[h] = tn(joins, table_sum[h].astype(BF16)).astype(BF16)
-
-
-def block_grads(last, core, blocks, rim, halves, gains, strips, row_label, col_label):
+    pack_grads(core_ref[0], g_qkv, g_proj, g_up, g_down, kept_ref, given_ref)
+    spread_rows = [tn(joins, table_sum[h].astype(BF16)) for h in range(HEADS)]
+    ends = jnp.concatenate([p[:, 128:] for p in spread_rows] + [jnp.zeros((192, 32), F32)], axis=1)
+    ends = ends + tn(gain_sums[...].astype(BF16), gain_lane)
+    for e in range(64):
+        at = slice(3 * e, 3 * e + 3)
+        piece = jnp.concatenate([p[at, :128] for p in spread_rows] + [ends[at]], axis=0)
+        strips_ref[e] = piece.astype(BF16)
+
+
+def block_grads(last, core, blocks, rim, halves, landed, row_label, col_label):
     rows = 4 * WIN
     out = [
         ((4, WIN, D), BF16),
         ((WIN, D), BF16),
-        ((2, 64, 27, 128), BF16),
-        ((2, D), F32),
-        ((HEADS, 192, WIN), BF16),
+        ((64, 27, 128), BF16),
+        ((64, 27, 128), BF16),
+        ((64, 21, 128), BF16),
     ]
     scratch = [
         ((3 * D, D), BF16),
@@ -296,7 +324,12 @@
         ((D, FFN), F32),
         ((4, WIN, 2 * D), F32),
         ((HEADS, WIN, WIN), F32),
-        ((HEADS, WIN, WIN), F32),
+        ((HEADS * WIN, WIN), F32),
+        ((HEADS * WIN, WIN), F32),
+        ((HEADS * WIN, WIN), BF16),
+        ((HEADS * WIN, WIN), BF16),
+        ((HEADS * WIN, D), BF16),
+        ((HEADS * WIN, D), BF16),
         ((HEADS, WIN, WIN), F32),
         ((rows, D), BF16),
         ((rows, D), BF16),
@@ -306,18 +339,18 @@
         ((rows, D), BF16),
         ((3, rows, D), BF16),
         ((4, WIN, D), F32),
-        ((2, D), F32),
+        ((8, D), F32),
     ]
     whole = pl.BlockSpec(memory_space=pltpu.VMEM)
     return pl.pallas_call(
         block_kernel,
-        in_specs=[pl.BlockSpec(memory_space=pltpu.SMEM)] * 2 + [whole] * 10,
+        in_specs=[pl.BlockSpec(memory_space=pltpu.SMEM)] * 2 + [whole] * 9,
         out_specs=[whole] * len(out),
         out_shape=[jax.ShapeDtypeStruct(s, t) for s, t in out],
         scratch_shapes=[pltpu.VMEM(s, t) for s, t in scratch],
         compiler_params=pltpu.CompilerParams(vmem_limit_bytes=48 << 20),
         name="block_grads",
-    )(last.reshape(1), core.reshape(1), *blocks, rim, halves, gains, strips, row_label, col_label)
+    )(last.reshape(1), core.reshape(1), *blocks, rim, halves, landed, row_label, col_label)
 
 
 def shards(
@@ -362,50 +395,41 @@
     slabs = slabs.reshape(positions, HEADS, own)
     slabs = lax.dynamic_update_slice(
         jnp.zeros((positions, HEADS, 3 * WIN), BF16), slabs, (0, 0, x_index * 36)
-    ).reshape(positions, -1)
-    slab_size = slabs.shape[1]
-    gain_part = jnp.broadcast_to(norm_gains.reshape(1, 6), (positions, 6))
-    fill = jnp.zeros((positions, 21 * 128 - slab_size - 6), BF16)
-    slabs = jnp.concatenate([slabs, gain_part, fill], axis=1).reshape(positions, 21, 128)
+    ).reshape(positions, HEADS, 3, WIN)
+    main = slabs[..., :128].reshape(positions, 18, 128)
+    ends = slabs[..., 128:].transpose(0, 2, 1, 3).reshape(positions, 3, 96)
+    gain_part = jnp.broadcast_to(norm_gains.T[None], (positions, 3, 2))
+    ends = jnp.concatenate([ends, gain_part, jnp.zeros((positions, 3, 30), BF16)], axis=2)
+    slabs = jnp.concatenate([main, ends], axis=1)
     parcel = jnp.concatenate([jnp.broadcast_to(half[None], (positions, 27, 128)), slabs], axis=1)
     parcel = jnp.broadcast_to(parcel[None], (groups, members, 48, 128)).reshape(lons, 48, 128)
-    parcel, cells = lax.optimization_barrier((parcel, cells))
+
     arrived = passed_along(cells[:, 0], LAT, -1)
-    landed = lax.all_to_all(parcel, LON, 0, 0)
-
-    halves = lax.all_gather(landed[:, :27], "core", axis=0)
-    tail = landed[:, 27:].reshape(lons, 21 * 128)
-    gains = tail[:, slab_size : slab_size + 6].reshape(lons, 2, 3).transpose(1, 0, 2).reshape(2, D)
-    strips = tail[:, :slab_size].reshape(lons, HEADS, 3, WIN).transpose(1, 0, 2, 3)
-    strips = strips.reshape(HEADS, 3 * lons, WIN)
-
+    parcel, arrived = lax.optimization_barrier((parcel, arrived))
     cells = jnp.concatenate([cells[:, 1], arrived], axis=1)
     cells = jnp.concatenate([cells, cells[: members - 1]], axis=0)
     cells = lax.dynamic_slice_in_dim(cells, x_index, members, 0)
     blocks = [cells[0]] + [passed_along(cells[k], ("x",), k) for k in range(1, members)]
+    landed = lax.all_to_all(parcel, LON, 0, 0)
     is_first = [x_index == k for k in range(members)]
     rim = blocks[0]
     for k in range(1, members):
         rim = jnp.where(is_first[k], blocks[k], rim)
     rim = passed_along(rim, ("yl", "z"), -1)
     last = (x_index + 1) % members
+    halves = lax.all_gather(landed[:, :27], "core", axis=0)
 
     labels = lax.dynamic_slice(region, (x_index * WPL, jnp.int32(0)), (WPL, WLAT))
     labels = jnp.broadcast_to(labels[:, :, None], (WPL, WLAT, WLON)).reshape(WIN)
-    back, rim, packed, g_gains, strips = block_grads(
-        last, core, blocks, rim, halves, gains, strips, labels.reshape(WIN, 1), labels.reshape(1, WIN)
+    back, rim, kept, given, strips = block_grads(
+        last, core, blocks, rim, halves, landed, labels.reshape(WIN, 1), labels.reshape(1, WIN)
     )
 
-    g_half = packed[0].astype(F32) + passed_along(packed[1], ("core",), 1).astype(F32)
-    g_half = g_half.astype(BF16)
-    strips = strips.reshape(HEADS, lons, 3, WIN).transpose(1, 0, 2, 3).reshape(lons, slab_size)
-    g_gain_part = g_gains.reshape(2, lons, 3).transpose(1, 0, 2).reshape(lons, 6).astype(BF16)
-    fill = jnp.zeros((lons, 21 * 128 - slab_size - 6), BF16)
-    strips = jnp.concatenate([strips, g_gain_part, fill], axis=1).reshape(lons, 21, 128)
-    parcel = jnp.concatenate([g_half, strips], axis=1)
+    g_half = kept.astype(F32) + passed_along(given, ("core",), 1).astype(F32)
+    parcel = jnp.concatenate([g_half.astype(BF16), strips], axis=1)
     parcel, rim = lax.optimization_barrier((parcel, rim))
+    rim = passed_along(rim, ("yl", "z"), 1)
     returned = lax.all_to_all(parcel, LON, 0, 0)
-    rim = passed_along(rim, ("yl", "z"), 1)
     blocks = [jnp.where(is_first[k], back[k] + rim, back[k]) for k in range(members)]
     blocks = [blocks[0]] + [passed_along(blocks[k], ("x",), -k) for k in range(1, members)]
     back = jnp.stack(blocks + blocks[: members - 1])
@@ -419,13 +443,13 @@
     returned = returned.astype(F32)
     half_sum = jnp.sum(returned[:, :27], axis=0).reshape(-1)
     half_size = half_sum.shape[0]
-    strip_sum = jnp.sum(returned[:, 27:].reshape(groups, members, 21 * 128), axis=0)
-    table_part = lax.dynamic_slice(
-        strip_sum[:, :slab_size].reshape(positions, HEADS, 3 * WIN),
-        (jnp.int32(0), jnp.int32(0), x_index * 36),
-        (positions, HEADS, own),
-    )
-    gain_sum = jnp.sum(strip_sum[:, slab_size : slab_size + 6], axis=0)
+    strip_sum = jnp.sum(returned[:, 27:].reshape(groups, members, 21, 128), axis=0)
+    ends = strip_sum[:, 18:, :96].reshape(positions, 3, HEADS, 16).transpose(0, 2, 1, 3)
+    table_part = jnp.concatenate(
+        [strip_sum[:, :18].reshape(positions, HEADS, 3, 128), ends], axis=3
+    ).reshape(positions, HEADS, 3 * WIN)
+    table_part = lax.dynamic_slice_in_dim(table_part, x_index * 36, own, 2)
+    gain_sum = jnp.sum(strip_sum[:, 18:, 96:98], axis=0).T.reshape(-1)
     note = jnp.concatenate([half_sum, table_part.reshape(-1), gain_sum])
     size = note.shape[0]
     note = jnp.pad(note.astype(BF16), (0, -size % 1024)).reshape(-1, 128)

time: 132 us -> 119 us (0.902)
  local copies, waits for them, and re-layouts: 22.4 us -> 10.6 us
  Pallas kernels: 20.2 us -> 17.4 us
  waiting for transfers between devices: 25.8 us -> 28.3 us
    reshape x10 -> x6, local copies, waits for them, and re-layouts: 5.02 us -> 0.39 us  [the longest x1 0.1 us: shards(): table_part = jnp.concatenate([strip_sum[:, :18].reshape(positions, HEADS,...]
    all_to_all x1, waiting for transfers between devices: 0.01 us -> 4.56 us  [shards(): landed = lax.all_to_all(parcel, LON, 0, 0)]
    ppermute x11, starting transfers between devices: 18.2 us -> 22.1 us  [passed_along(): lax.ppermute(block, axes, [((i - distance) % size, i) for i in range(size)])]
    pallas_call x1, Pallas kernels: 20.2 us -> 17.4 us  [block_grads(): pl.pallas_call(block_kernel, in_specs=[pl.BlockSpec(memory_space=pltpu.SM...]
    ppermute x11, waiting for transfers between devices: 25 us -> 22.4 us  [passed_along(): lax.ppermute(block, axes, [((i - distance) % size, i) for i in range(size)])]
    transpose x3 -> x4, local copies, waits for them, and re-layouts: 2.72 us -> 0.23 us  [the longest x1 0.11 us: shards(): gain_part = jnp.broadcast_to(norm_gains.T[None], (positions, 3, 2))]
    all_to_all x1, starting transfers between devices: 8.59 us -> 6.78 us  [shards(): returned = lax.all_to_all(parcel, LON, 0, 0)]
    all_to_all x1, starting transfers between devices: 14.1 us -> 12.4 us  [shards(): landed = lax.all_to_all(parcel, LON, 0, 0)]
  transfers between devices with their start and end apart: 13 -> 13, of which waited for: 8 -> 11; matrix products, arithmetic and copies ran while one was open for 9% -> 5% of each run, Pallas kernels for 0% -> 0%
where the time goes in v1:
time: 119 us
  starting transfers between devices  41.3 us (35%)
  waiting for transfers between devices  28.3 us (24%)
  Pallas kernels  17.4 us (15%)
  blocking collectives  11.8 us (10%)
  local copies, waits for them, and re-layouts  10.6 us (9%)
  other arithmetic  7.09 us (6%)
  between operations  1.38 us (1%)
    ppermute x11, waiting for transfers between devices, passed_along(): lax.ppermute(block, axes, [((i - distance) % size, i) for i in range(size)])  22.4 us
    ppermute x11, starting transfers between devices, passed_along(): lax.ppermute(block, axes, [((i - distance) % size, i) for i in range(size)])  22.1 us
    pallas_call x1, Pallas kernels, block_grads(): pl.pallas_call(block_kernel, in_specs=[pl.BlockSpec(memory_space=pltpu.SM...  17.4 us
    all_to_all x1, starting transfers between devices, shards(): landed = lax.all_to_all(parcel, LON, 0, 0)  12.4 us
    all_gather x1, blocking collectives, shards(): notes = lax.all_gather(note, LAT, axis=0).astype(F32).reshape(4, -1)  9.23 us
    all_to_all x1, starting transfers between devices, shards(): returned = lax.all_to_all(parcel, LON, 0, 0)  6.78 us
    all_to_all x1, waiting for transfers between devices, shards(): landed = lax.all_to_all(parcel, LON, 0, 0)  4.56 us
    all_gather x1, blocking collectives, shards(): halves = lax.all_gather(landed[:, :27], 'core', axis=0)  2.62 us
  transfers between devices with their start and end apart: 13, of which 11 were waited for; matrix products, arithmetic and copies ran while one was open for 5% of the time, Pallas kernels for 0%

profile of v1, /device:TPU:1, one launch (start us, length us, event | category | flops | bytes accessed | tf_op | source)
XLA Modules:
  0.0 118.9 jit_solution(1652995832550158585)
XLA Ops:
  0.6 1.3 %slice_maximum_fusion = bf16[7,6,12,384]{3,0,2,1:T(8,128)(2,1)S(1)} fusion(bf16[8,6,12,192]{3,0,2,1:T(8,128)(2,1)} %param.11, bf16[8,6,12,192]{3,0,2,1:T(8,128)(2,1)} %param.10), kind=kLoop, calls=%fused_computation.13 | loop fusion | flops 774144 | bytes 829440 | tf_op jit(solution)/shard_map/concatenate | solution.py:378
  1.9 1.4 %fusion.3 = bf16[8,6,12,384]{3,0,2,1:T(8,128)(2,1)S(1)} fusion(bf16[8,6,12,192]{3,0,2,1:T(8,128)(2,1)} %param.11, bf16[8,6,12,192]{3,0,2,1:T(8,128)(2,1)} %param.10, bf16[7,6,12,384]{3,0,2,1:T(8,128)(2,1)S(1)} %slice_maximum_fusion), kind=kLoop, calls=%fused_computation.12 | loop fusion | flops 1327104 | bytes 1271808 | tf_op jit(solution)/shard_map/jit(_roll_static)/concatenate | solution.py:379
  4.6 3.3 %collective-permute-start = (bf16[4,72,384]{2,1,0:T(8,128)(2,1)S(1)}, bf16[4,72,384]{2,1,0:T(8,128)(2,1)S(1)}, u32[]{:S(2)}, u32[]{:S(2)}) collective-permute-start(bf16[4,72,384]{2,1,0:T(8,128)(2,1)S(1)} %bitcast.150), channel_id=1, source_target_pairs={{64,0},{128,64},{192,128},{0,192},{65,1},{129,65},{193,129},{1,193... | collective-permute-start | bytes 663560 | tf_op jit(solution)/shard_map/ppermute | solution.py:26
  10.1 2.4 %collective-permute-done = bf16[4,72,384]{2,1,0:T(8,128)(2,1)S(1)} collective-permute-done((bf16[4,72,384]{2,1,0:T(8,128)(2,1)S(1)}, bf16[4,72,384]{2,1,0:T(8,128)(2,1)S(1)}, u32[]{:S(2)}, u32[]{:S(2)}) %collective-permute-start) | collective-permute-done | bytes 221216 | tf_op jit(solution)/shard_map/ppermute | solution.py:26
  12.6 1.1 broadcast_in_dim.19
  13.6 12.4 %all-to-all-start = ((bf16[64,48,128]{2,1,0:T(8,128)(2,1)}), bf16[64,48,128]{2,1,0:T(8,128)(2,1)S(1)}, u32[]{:S(2)}, u32[]{:S(2)}) async-start(bf16[64,48,128]{2,1,0:T(8,128)(2,1)} %bitcast.19), calls=%async_computation | async-start | bytes 1572864 | tf_op jit(solution)/shard_map/all_to_all | solution.py:413
  26.1 0.7 fusion.1
  26.9 1.1 collective-permute-start.1
  28.0 2.4 %collective-permute-start.2 = (bf16[144,384]{1,0:T(8,128)(2,1)S(1)}, bf16[144,384]{1,0:T(8,128)(2,1)S(1)}, u32[]{:S(2)}, u32[]{:S(2)}) collective-permute-start(bf16[144,384]{1,0:T(8,128)(2,1)S(1)} %get-tuple-element.26), channel_id=1, source_target_pairs={{2,0},{3,1},{0,2},{1,3},{6,4},{7,5},{4,6},{5,7},{10,8},{11,9},{8,1... | collective-permute-start | bytes 331784 | tf_op jit(solution)/shard_map/ppermute | solution.py:26
  30.4 1.2 collective-permute-start.3
  31.8 2.5 %collective-permute-done.1.b1 = bf16[144,384]{1,0:T(8,128)(2,1)S(1)} collective-permute-done((bf16[144,384]{1,0:T(8,128)(2,1)S(1)}, bf16[144,384]{1,0:T(8,128)(2,1)S(1)}, u32[]{:S(2)}, u32[]{:S(2)}) %collective-permute-start.1) | collective-permute-done | bytes 110624 | tf_op jit(solution)/shard_map/ppermute | solution.py:26
  34.4 5.0 %collective-permute-done.2.b2 = bf16[144,384]{1,0:T(8,128)(2,1)S(1)} collective-permute-done((bf16[144,384]{1,0:T(8,128)(2,1)S(1)}, bf16[144,384]{1,0:T(8,128)(2,1)S(1)}, u32[]{:S(2)}, u32[]{:S(2)}) %collective-permute-start.2) | collective-permute-done | bytes 110624 | tf_op jit(solution)/shard_map/ppermute | solution.py:26
  39.8 4.8 %collective-permute-start.4 = (bf16[144,384]{1,0:T(8,128)(2,1)S(1)}, bf16[144,384]{1,0:T(8,128)(2,1)S(1)}, u32[]{:S(2)}, u32[]{:S(2)}) collective-permute-start(bf16[144,384]{1,0:T(8,128)(2,1)S(1)} %select_select_fusion), channel_id=1, source_target_pairs={{4,0},{8,4},{12,8},{16,12},{20,16},{24,20},{28,24},{32,28},{36,32}... | collective-permute-start | bytes 331784 | tf_op jit(solution)/shard_map/ppermute | solution.py:26
  44.7 4.6 %all-to-all-done.landed_ref = bf16[64,48,128]{2,1,0:T(8,128)(2,1)S(1)} async-done(((bf16[64,48,128]{2,1,0:T(8,128)(2,1)}), bf16[64,48,128]{2,1,0:T(8,128)(2,1)S(1)}, u32[]{:S(2)}, u32[]{:S(2)}) %all-to-all-start) | async-done | bytes 786464 | tf_op jit(solution)/shard_map/all_to_all | solution.py:413
  49.5 2.6 %all-gather = bf16[128,27,128]{2,0,1:T(8,128)(2,1)S(1)} all-gather(bf16[64,27,128]{2,0,1:T(8,128)(2,1)S(1)} %copy.99), channel_id=2, replica_groups=mesh['yh'=2,'core'=2,'yl'=2,'z'=8,'x'=4] {'core'}, dimensions={0}, use_global_device_ids=true | all-gather | bytes 1327104 | tf_op jit(solution)/shard_map/all_gather | solution.py:420
  52.7 17.4 %block_grads.1 = (bf16[4,144,192]{2,1,0:T(8,128)(2,1)S(1)}, bf16[144,192]{1,0:T(8,128)(2,1)S(1)}, bf16[64,27,128]{2,1,0:T(8,128)(2,1)S(1)}, bf16[64,27,128]{2,1,0:T(8,128)(2,1)S(1)}, bf16[64,21,128]{2,1,0:T(8,128)(2,1)S(1)}) custom-call(s32[1]{0:T(128)} %bitcast.last_ref, s32[1]{0:T(128)} %bitcast.1.core_ref, bf16[144,384]{1,0:T(8,128)(2,1)S(1)} %get-tuple-element.28.b0, ...), custom_call_target="tpu_custom_call" | custom-call | tf_op jit(solution)/shard_map/block_grads/pallas_call | solution.py:345
  70.3 1.8 %collective-permute-done.5 = bf16[64,27,128]{2,1,0:T(8,128)(2,1)S(1)} collective-permute-done((bf16[64,27,128]{2,1,0:T(8,128)(2,1)S(1)}, bf16[64,27,128]{2,1,0:T(8,128)(2,1)S(1)}, u32[]{:S(2)}, u32[]{:S(2)}) %collective-permute-start.5) | collective-permute-done | bytes 442400 | tf_op jit(solution)/shard_map/ppermute | solution.py:26
  72.2 1.1 pad_maximum_fusion
  73.3 1.4 %collective-permute-start.6 = (bf16[144,192]{1,0:T(8,128)(2,1)S(1)}, bf16[144,192]{1,0:T(8,128)(2,1)S(1)}, u32[]{:S(2)}, u32[]{:S(2)}) collective-permute-start(bf16[144,192]{1,0:T(8,128)(2,1)S(1)} %get-tuple-element.23), channel_id=1, source_target_pairs={{60,0},{0,4},{4,8},{8,12},{12,16},{16,20},{20,24},{24,28},{28,32},... | collective-permute-start | bytes 165896 | tf_op jit(solution)/shard_map/ppermute | solution.py:26
  74.8 6.8 %all-to-all-start.1 = ((bf16[64,48,128]{2,1,0:T(8,128)(2,1)}), bf16[64,48,128]{2,1,0:T(8,128)(2,1)S(1)}, u32[]{:S(2)}, u32[]{:S(2)}) async-start(bf16[64,48,128]{2,1,0:T(8,128)(2,1)} %pad_maximum_fusion), calls=%async_computation.1 | async-start | bytes 1572864 | tf_op jit(solution)/shard_map/all_to_all | solution.py:432
  81.6 2.3 %collective-permute-start.7 = (bf16[144,192]{1,0:T(8,128)(2,1)S(1)}, bf16[144,192]{1,0:T(8,128)(2,1)S(1)}, u32[]{:S(2)}, u32[]{:S(2)}) collective-permute-start(bf16[144,192]{1,0:T(8,128)(2,1)S(1)} %get-tuple-element.33), channel_id=1, source_target_pairs={{1,0},{2,1},{3,2},{0,3},{5,4},{6,5},{7,6},{4,7},{9,8},{10,9},{11,1... | collective-permute-start | bytes 165896 | tf_op jit(solution)/shard_map/ppermute | solution.py:26
  85.1 0.7 collective-permute-done.7
  85.8 3.6 %collective-permute-done.8 = bf16[144,192]{1,0:T(8,128)(2,1)S(1)} collective-permute-done((bf16[144,192]{1,0:T(8,128)(2,1)S(1)}, bf16[144,192]{1,0:T(8,128)(2,1)S(1)}, u32[]{:S(2)}, u32[]{:S(2)}) %collective-permute-start.8) | collective-permute-done | bytes 55328 | tf_op jit(solution)/shard_map/ppermute | solution.py:26
  89.3 2.4 %collective-permute-done.9 = bf16[144,192]{1,0:T(8,128)(2,1)S(1)} collective-permute-done((bf16[144,192]{1,0:T(8,128)(2,1)S(1)}, bf16[144,192]{1,0:T(8,128)(2,1)S(1)}, u32[]{:S(2)}, u32[]{:S(2)}) %collective-permute-start.9) | collective-permute-done | bytes 55328 | tf_op jit(solution)/shard_map/ppermute | solution.py:26
  91.8 4.2 %collective-permute-start.10 = (bf16[4,72,192]{2,1,0:T(8,128)(2,1)S(1)}, bf16[4,72,192]{2,1,0:T(8,128)(2,1)S(1)}, u32[]{:S(2)}, u32[]{:S(2)}) collective-permute-start(bf16[4,72,192]{2,1,0:T(8,128)(2,1)S(1)} %get-tuple-element.34), channel_id=1, source_target_pairs={{192,0},{0,64},{64,128},{128,192},{193,1},{1,65},{65,129},{129,193... | collective-permute-start | bytes 331784 | tf_op jit(solution)/shard_map/ppermute | solution.py:26
  96.3 3.6 %collective-permute-done.10 = bf16[4,72,192]{2,1,0:T(8,128)(2,1)S(1)} collective-permute-done((bf16[4,72,192]{2,1,0:T(8,128)(2,1)S(1)}, bf16[4,72,192]{2,1,0:T(8,128)(2,1)S(1)}, u32[]{:S(2)}, u32[]{:S(2)}) %collective-permute-start.10) | collective-permute-done | bytes 110624 | tf_op jit(solution)/shard_map/ppermute | solution.py:26
  100.8 0.9 pad_maximum_fusion.2
  101.7 1.3 %all-to-all-done.1 = bf16[64,48,128]{2,1,0:T(8,128)(2,1)S(1)} async-done(((bf16[64,48,128]{2,1,0:T(8,128)(2,1)}), bf16[64,48,128]{2,1,0:T(8,128)(2,1)S(1)}, u32[]{:S(2)}, u32[]{:S(2)}) %all-to-all-start.1) | async-done | bytes 786464 | tf_op jit(solution)/shard_map/all_to_all | solution.py:432
  104.3 9.2 %all_gather.11 = bf16[4,88,128]{2,1,0:T(8,128)(2,1)S(1)} all-gather(bf16[1,88,128]{2,1,0:T(8,128)(2,1)S(1)} %pad_bitcast_fusion), channel_id=1, replica_groups=mesh['yh'=2,'core'=2,'yl'=2,'z'=8,'x'=4] {'yh','core'}, dimensions={0}, use_global_device_ids=true | all-gather | bytes 112640 | tf_op jit(solution)/shard_map/all_gather | solution.py:456
  115.5 0.9 reshape.170
  116.8 0.6 mul.28
  117.5 0.8 fusion.5
  (147 shorter events, 11.7 us)
Async XLA Ops:
  0.6 30.9 %copy-start = (s32[8,6]{1,0:T(8,128)S(1)}, s32[8,6]{1,0:T(8,128)}, u32[]{:S(2)}) copy-start(s32[8,6]{1,0:T(8,128)} %param.19) | copy-start | bytes 580
  3.5 4.4 %copy-start.1 = (bf16[16,6,324]{2,0,1:T(8,128)(2,1)S(1)}, bf16[16,6,324]{2,0,1:T(8,128)(2,1)}, u32[]{:S(2)}) copy-start(bf16[16,6,324]{2,0,1:T(8,128)(2,1)} %param.17) | copy-start | bytes 186628
  3.8 4.2 %copy-start.4 = (s32[4,4]{1,0:T(4,128)S(1)}, s32[4,4]{1,0:T(4,128)}, u32[]{:S(2)}) copy-start(s32[4,4]{1,0:T(4,128)} %param.18) | copy-start | bytes 196
  3.8 5.1 %copy-start.2 = (bf16[192,12]{0,1:T(8,128)(2,1)S(1)}, bf16[192,12]{0,1:T(8,128)(2,1)}, u32[]{:S(2)}) copy-start(bf16[192,12]{0,1:T(8,128)(2,1)} %param.14) | copy-start | bytes 13828
  3.9 5.1 %copy-start.3 = (bf16[192,9]{0,1:T(8,128)(2,1)S(1)}, bf16[192,9]{0,1:T(8,128)(2,1)}, u32[]{:S(2)}) copy-start(bf16[192,9]{0,1:T(8,128)(2,1)} %param.12) | copy-start | bytes 10372
  3.9 5.1 %copy-start.6 = (bf16[192,3]{0,1:T(4,128)(2,1)S(1)}, bf16[192,3]{0,1:T(4,128)(2,1)}, u32[]{:S(2)}) copy-start(bf16[192,3]{0,1:T(4,128)(2,1)} %param.13) | copy-start | bytes 3460
  3.9 5.3 %copy-start.7 = (bf16[2,3]{1,0:T(2,128)(2,1)S(1)}, bf16[2,3]{1,0:T(2,128)(2,1)}, u32[]{:S(2)}) copy-start(bf16[2,3]{1,0:T(2,128)(2,1)} %param.16) | copy-start | bytes 40
  3.9 5.7 %copy-start.5 = (bf16[768,3]{0,1:T(4,128)(2,1)S(1)}, bf16[768,3]{0,1:T(4,128)(2,1)}, u32[]{:S(2)}) copy-start(bf16[768,3]{0,1:T(4,128)(2,1)} %param.15) | copy-start | bytes 13828
  4.6 8.0 %collective-permute-start = (bf16[4,72,384]{2,1,0:T(8,128)(2,1)S(1)}, bf16[4,72,384]{2,1,0:T(8,128)(2,1)S(1)}, u32[]{:S(2)}, u32[]{:S(2)}) collective-permute-start(bf16[4,72,384]{2,1,0:T(8,128)(2,1)S(1)} %bitcast.150), channel_id=1, source_target_pairs={{64,0},{128,64},{192,128},{0,192},{65,1},{129,65},{193,129},{1,193... | collective-permute-start | bytes 663560 | tf_op jit(solution)/shard_map/ppermute | solution.py:26
  13.6 35.6 %all-to-all-start = ((bf16[64,48,128]{2,1,0:T(8,128)(2,1)}), bf16[64,48,128]{2,1,0:T(8,128)(2,1)S(1)}, u32[]{:S(2)}, u32[]{:S(2)}) async-start(bf16[64,48,128]{2,1,0:T(8,128)(2,1)} %bitcast.19), calls=%async_computation | async-start | bytes 1572864 | tf_op jit(solution)/shard_map/all_to_all | solution.py:413
  26.9 7.5 %collective-permute-start.1 = (bf16[144,384]{1,0:T(8,128)(2,1)S(1)}, bf16[144,384]{1,0:T(8,128)(2,1)S(1)}, u32[]{:S(2)}, u32[]{:S(2)}) collective-permute-start(bf16[144,384]{1,0:T(8,128)(2,1)S(1)} %get-tuple-element.27), channel_id=1, source_target_pairs={{3,0},{0,1},{1,2},{2,3},{7,4},{4,5},{5,6},{6,7},{11,8},{8,9},{9,10... | collective-permute-start | bytes 331784 | tf_op jit(solution)/shard_map/ppermute | solution.py:26
  28.0 11.4 %collective-permute-start.2 = (bf16[144,384]{1,0:T(8,128)(2,1)S(1)}, bf16[144,384]{1,0:T(8,128)(2,1)S(1)}, u32[]{:S(2)}, u32[]{:S(2)}) collective-permute-start(bf16[144,384]{1,0:T(8,128)(2,1)S(1)} %get-tuple-element.26), channel_id=1, source_target_pairs={{2,0},{3,1},{0,2},{1,3},{6,4},{7,5},{4,6},{5,7},{10,8},{11,9},{8,1... | collective-permute-start | bytes 331784 | tf_op jit(solution)/shard_map/ppermute | solution.py:26
  30.4 9.4 %collective-permute-start.3 = (bf16[144,384]{1,0:T(8,128)(2,1)S(1)}, bf16[144,384]{1,0:T(8,128)(2,1)S(1)}, u32[]{:S(2)}, u32[]{:S(2)}) collective-permute-start(bf16[144,384]{1,0:T(8,128)(2,1)S(1)} %get-tuple-element.25), channel_id=1, source_target_pairs={{1,0},{2,1},{3,2},{0,3},{5,4},{6,5},{7,6},{4,7},{9,8},{10,9},{11,1... | collective-permute-start | bytes 331784 | tf_op jit(solution)/shard_map/ppermute | solution.py:26
  39.8 12.8 %collective-permute-start.4 = (bf16[144,384]{1,0:T(8,128)(2,1)S(1)}, bf16[144,384]{1,0:T(8,128)(2,1)S(1)}, u32[]{:S(2)}, u32[]{:S(2)}) collective-permute-start(bf16[144,384]{1,0:T(8,128)(2,1)S(1)} %select_select_fusion), channel_id=1, source_target_pairs={{4,0},{8,4},{12,8},{16,12},{20,16},{24,20},{28,24},{32,28},{36,32}... | collective-permute-start | bytes 331784 | tf_op jit(solution)/shard_map/ppermute | solution.py:26
  70.1 2.0 %collective-permute-start.5 = (bf16[64,27,128]{2,1,0:T(8,128)(2,1)S(1)}, bf16[64,27,128]{2,1,0:T(8,128)(2,1)S(1)}, u32[]{:S(2)}, u32[]{:S(2)}) collective-permute-start(bf16[64,27,128]{2,1,0:T(8,128)(2,1)S(1)} %get-tuple-element.20), channel_id=1, source_target_pairs={{64,0},{0,64},{65,1},{1,65},{66,2},{2,66},{67,3},{3,67},{68,4},{4,... | collective-permute-start | bytes 1327112 | tf_op jit(solution)/shard_map/ppermute | solution.py:26
  73.3 8.2 %collective-permute-start.6 = (bf16[144,192]{1,0:T(8,128)(2,1)S(1)}, bf16[144,192]{1,0:T(8,128)(2,1)S(1)}, u32[]{:S(2)}, u32[]{:S(2)}) collective-permute-start(bf16[144,192]{1,0:T(8,128)(2,1)S(1)} %get-tuple-element.23), channel_id=1, source_target_pairs={{60,0},{0,4},{4,8},{8,12},{12,16},{16,20},{20,24},{24,28},{28,32},... | collective-permute-start | bytes 165896 | tf_op jit(solution)/shard_map/ppermute | solution.py:26
  74.8 28.2 %all-to-all-start.1 = ((bf16[64,48,128]{2,1,0:T(8,128)(2,1)}), bf16[64,48,128]{2,1,0:T(8,128)(2,1)S(1)}, u32[]{:S(2)}, u32[]{:S(2)}) async-start(bf16[64,48,128]{2,1,0:T(8,128)(2,1)} %pad_maximum_fusion), calls=%async_computation.1 | async-start | bytes 1572864 | tf_op jit(solution)/shard_map/all_to_all | solution.py:432
  81.6 4.1 %collective-permute-start.7 = (bf16[144,192]{1,0:T(8,128)(2,1)S(1)}, bf16[144,192]{1,0:T(8,128)(2,1)S(1)}, u32[]{:S(2)}, u32[]{:S(2)}) collective-permute-start(bf16[144,192]{1,0:T(8,128)(2,1)S(1)} %get-tuple-element.33), channel_id=1, source_target_pairs={{1,0},{2,1},{3,2},{0,3},{5,4},{6,5},{7,6},{4,7},{9,8},{10,9},{11,1... | collective-permute-start | bytes 165896 | tf_op jit(solution)/shard_map/ppermute | solution.py:26
  83.9 5.4 %collective-permute-start.8 = (bf16[144,192]{1,0:T(8,128)(2,1)S(1)}, bf16[144,192]{1,0:T(8,128)(2,1)S(1)}, u32[]{:S(2)}, u32[]{:S(2)}) collective-permute-start(bf16[144,192]{1,0:T(8,128)(2,1)S(1)} %get-tuple-element.32), channel_id=1, source_target_pairs={{2,0},{3,1},{0,2},{1,3},{6,4},{7,5},{4,6},{5,7},{10,8},{11,9},{8,1... | collective-permute-start | bytes 165896 | tf_op jit(solution)/shard_map/ppermute | solution.py:26
  84.5 7.2 %collective-permute-start.9 = (bf16[144,192]{1,0:T(8,128)(2,1)S(1)}, bf16[144,192]{1,0:T(8,128)(2,1)S(1)}, u32[]{:S(2)}, u32[]{:S(2)}) collective-permute-start(bf16[144,192]{1,0:T(8,128)(2,1)S(1)} %get-tuple-element.31), channel_id=1, source_target_pairs={{3,0},{0,1},{1,2},{2,3},{7,4},{4,5},{5,6},{6,7},{11,8},{8,9},{9,10... | collective-permute-start | bytes 165896 | tf_op jit(solution)/shard_map/ppermute | solution.py:26
  91.8 8.0 %collective-permute-start.10 = (bf16[4,72,192]{2,1,0:T(8,128)(2,1)S(1)}, bf16[4,72,192]{2,1,0:T(8,128)(2,1)S(1)}, u32[]{:S(2)}, u32[]{:S(2)}) collective-permute-start(bf16[4,72,192]{2,1,0:T(8,128)(2,1)S(1)} %get-tuple-element.34), channel_id=1, source_target_pairs={{192,0},{0,64},{64,128},{128,192},{193,1},{1,65},{65,129},{129,193... | collective-permute-start | bytes 331784 | tf_op jit(solution)/shard_map/ppermute | solution.py:26

commit v2 on v1

--- a/solution.py
+++ b/solution.py
@@ -1,3 +1,4 @@
+import functools
 import math
 
 import jax
@@ -353,6 +354,117 @@
     )(last.reshape(1), core.reshape(1), *blocks, rim, halves, landed, row_label, col_label)
 
 
+def one_hot(mask):
+    return mask.astype(F32).astype(BF16)
+
+
+def iota2(shape, axis):
+    return lax.broadcasted_iota(jnp.int32, shape, axis)
+
+
+def pack_kernel(
+    spot_ref, types_ref, qkv_ref, proj_ref, up_ref, down_ref, gains_ref, table_ref, out_ref
+):
+    x_index, core, lat = spot_ref[0], spot_ref[1], spot_ref[2]
+
+    first = up_ref[...].astype(F32)
+    second = jnp.concatenate([qkv_ref[...].astype(F32), proj_ref[...].astype(F32)], axis=0)
+    halves = []
+    for rows in (first, second):
+        rows = jnp.where(core == 0, rows[:6], rows[6:])
+        halves.append(rows[:, :128])
+        halves.append(jnp.concatenate([rows[:3, 128:], rows[3:, 128:]], axis=1))
+    unit = iota2((1, 384), 1)
+    unit = 12 * (unit // 6) + unit % 6 + 6 * core
+    chosen = one_hot(iota2((FFN, 384), 0) == unit)
+    downs = nn(down_ref[...], chosen)
+    downs = [downs[:, 128 * t : 128 * (t + 1)] for t in range(3)]
+    half = halves[:2] + downs + halves[2:]
+    spots = one_hot(iota2((2, 128), 1) == 96 + iota2((2, 128), 0))
+    gain_ends = tn(gains_ref[...], spots)
+    wanted = jnp.full((8, 16), -1, jnp.int32)
+    for a in range(4):
+        wanted = jnp.where(iota2((8, 16), 0) == a, types_ref[a, lat], wanted)
+    wanted = one_hot(iota2((8, 16), 1) == wanted)
+    slabs = []
+    for h in range(HEADS):
+        slab = nn(wanted, table_ref[h])
+        slab = jnp.concatenate([slab, jnp.zeros((8, 512 - 324), F32)], axis=1)
+        slabs.append(pltpu.roll(slab, x_index * 36, 1))
+    for a in range(4):
+        slab = jnp.concatenate([p[a : a + 1] for p in slabs], axis=0)
+        mains = [slab[:, WIN * r : WIN * r + 128] for r in range(3)]
+        mains = [m[h : h + 1] for h in range(HEADS) for m in mains]
+        ends = []
+        for r in range(3):
+            end = slab[:, WIN * r + 128 : WIN * (r + 1)]
+            ends.append(jnp.concatenate([end[h : h + 1] for h in range(HEADS)], axis=1))
+        ends = jnp.concatenate([jnp.concatenate(ends, axis=0), jnp.zeros((3, 32), F32)], axis=1)
+        piece = jnp.concatenate(half + mains + [ends + gain_ends], axis=0).astype(BF16)
+        for g in range(16):
+            out_ref[4 * g + a] = piece
+
+
+def finish_kernel(
+    factor, types_ref, notes_ref, qkv_ref, proj_ref, up_ref, down_ref, gains_ref, table_ref
+):
+    notes = [notes_ref[i, :32, :].astype(F32) for i in range(4)]
+
+    def six(note, at):
+        ends = [note[at + 6 : at + 9, :64], note[at + 6 : at + 9, 64:]]
+        return jnp.concatenate([note[at : at + 6], jnp.concatenate(ends, axis=0)], axis=1)
+
+    sums = [(notes[c] + notes[2 + c]) * factor for c in range(2)]
+    up_ref[:6, :] = six(sums[0], 0)
+    up_ref[6:, :] = six(sums[1], 0)
+    rest = six(sums[1], 18)
+    qkv_ref[:6, :] = six(sums[0], 18)
+    qkv_ref[6:, :] = rest[:3]
+    proj_ref[...] = rest[3:]
+    unit = iota2((1, 384), 1)
+    unit = 12 * (unit // 6) + unit % 6
+    downs = jnp.zeros((3, FFN), F32)
+    for c in range(2):
+        parts = []
+        for note in (notes[c], notes[2 + c]):
+            parts.append(
+                jnp.concatenate([note[9 + 3 * t : 12 + 3 * t] for t in range(3)], axis=1)
+            )
+        parts = jnp.concatenate(parts, axis=0).astype(BF16)
+        placed = nt(parts, one_hot(iota2((FFN, 384), 0) == unit + 6 * c))
+        downs = downs + (placed[:3] + placed[3:])
+    down_ref[...] = downs * factor
+    gains = (notes[0] + notes[1] + notes[2] + notes[3])[27:28] * factor
+    gains_ref[0:1, :] = gains[:, :3]
+    gains_ref[1:2, :] = gains[:, 3:6]
+    wanted = jnp.zeros((16, 16), jnp.int32)
+    for i in range(4):
+        for a in range(4):
+            wanted = jnp.where(iota2((16, 16), 1) == 4 * i + a, types_ref[a, i], wanted)
+    wanted = one_hot(iota2((16, 16), 0) == wanted)
+    tables = [notes_ref[i, 32:104, :].astype(F32) for i in range(4)]
+    for h in range(HEADS):
+        lanes = []
+        for j in range(3):
+            at = 4 * (3 * h + j)
+            terms = jnp.concatenate([t[at : at + 4] for t in tables], axis=0).astype(BF16)
+            lanes.append(nn(wanted, terms))
+        table_ref[h] = jnp.concatenate(lanes, axis=1)[:, :324]
+
+
+def small_call(kernel, args, scalars, out, scratch, name):
+    whole = pl.BlockSpec(memory_space=pltpu.VMEM)
+    flat = pl.BlockSpec(memory_space=pltpu.SMEM)
+    return pl.pallas_call(
+        kernel,
+        in_specs=[flat] * scalars + [whole] * (len(args) - scalars),
+        out_specs=[whole] * len(out),
+        out_shape=[jax.ShapeDtypeStruct(s, t) for s, t in out],
+        scratch_shapes=[pltpu.VMEM(s, t) for s, t in scratch],
+        name=name,
+    )(*args)
+
+
 def shards(
     inputs,
     cotangent,
@@ -379,30 +491,12 @@
     cells = jnp.roll(cells, -1, axis=0).reshape(positions, WPL, 2, WLAT // 2, WLON, 2 * D)
     cells = cells.transpose(0, 2, 1, 3, 4, 5).reshape(positions, 2, WIN // 2, 2 * D)
 
-    rows = jnp.concatenate([qkv_weight.T, proj_weight.T], axis=0)
-    rows = jnp.stack([up_weight.T.reshape(2, 6, D), rows.reshape(2, 6, D)], axis=1)
-    ends = rows[..., 128:].reshape(2, 2, 2, 3, 64).transpose(0, 1, 3, 2, 4).reshape(2, 2, 3, 128)
-    downs = down_weight.reshape(lons, 2, 6, 3).transpose(1, 3, 0, 2).reshape(2, 3, 3, 128)
-    downs = downs.transpose(0, 2, 1, 3).reshape(2, 9, 128)
-    both = jnp.concatenate([rows[..., :128], ends], axis=2)
-    half = jnp.concatenate([both[:, 0], downs, both[:, 1]], axis=1)
-    half = lax.dynamic_index_in_dim(half, core, 0, False)
-    types = lax.dynamic_slice(type_of, (jnp.int32(0), lat_index), (positions, 1))[:, 0]
-    onehot = types[:, None] == jnp.arange(type_count, dtype=jnp.int32)[None, :]
-    slabs = jnp.dot(
-        onehot.astype(BF16), bias_table.reshape(type_count, -1), preferred_element_type=F32
-    ).astype(BF16)
-    slabs = slabs.reshape(positions, HEADS, own)
-    slabs = lax.dynamic_update_slice(
-        jnp.zeros((positions, HEADS, 3 * WIN), BF16), slabs, (0, 0, x_index * 36)
-    ).reshape(positions, HEADS, 3, WIN)
-    main = slabs[..., :128].reshape(positions, 18, 128)
-    ends = slabs[..., 128:].transpose(0, 2, 1, 3).reshape(positions, 3, 96)
-    gain_part = jnp.broadcast_to(norm_gains.T[None], (positions, 3, 2))
-    ends = jnp.concatenate([ends, gain_part, jnp.zeros((positions, 3, 30), BF16)], axis=2)
-    slabs = jnp.concatenate([main, ends], axis=1)
-    parcel = jnp.concatenate([jnp.broadcast_to(half[None], (positions, 27, 128)), slabs], axis=1)
-    parcel = jnp.broadcast_to(parcel[None], (groups, members, 48, 128)).reshape(lons, 48, 128)
+    spot = jnp.stack([x_index, core, lat_index]).astype(jnp.int32)
+    weights = [w.T for w in (qkv_weight, proj_weight, up_weight, down_weight)]
+    weights += [norm_gains, bias_table.transpose(1, 0, 2)]
+    (parcel,) = small_call(
+        pack_kernel, (spot, type_of, *weights), 2, [((lons, 48, 128), BF16)], [], "pack"
+    )
 
     arrived = passed_along(cells[:, 0], LAT, -1)
     parcel, arrived = lax.optimization_barrier((parcel, arrived))
@@ -441,8 +535,7 @@
     grad_input = jnp.roll(back.reshape(inputs.shape), 1, axis=0)
 
     returned = returned.astype(F32)
-    half_sum = jnp.sum(returned[:, :27], axis=0).reshape(-1)
-    half_size = half_sum.shape[0]
+    half_sum = jnp.sum(returned[:, :27], axis=0)
     strip_sum = jnp.sum(returned[:, 27:].reshape(groups, members, 21, 128), axis=0)
     ends = strip_sum[:, 18:, :96].reshape(positions, 3, HEADS, 16).transpose(0, 2, 1, 3)
     table_part = jnp.concatenate(
@@ -450,40 +543,19 @@
     ).reshape(positions, HEADS, 3 * WIN)
     table_part = lax.dynamic_slice_in_dim(table_part, x_index * 36, own, 2)
     gain_sum = jnp.sum(strip_sum[:, 18:, 96:98], axis=0).T.reshape(-1)
-    note = jnp.concatenate([half_sum, table_part.reshape(-1), gain_sum])
-    size = note.shape[0]
-    note = jnp.pad(note.astype(BF16), (0, -size % 1024)).reshape(-1, 128)
-    notes = lax.all_gather(note, LAT, axis=0).astype(F32).reshape(4, -1)
-    whole = jnp.sum(notes[:, :half_size].reshape(2, 2, 27, 128), axis=0)
-    table_size = positions * HEADS * own
-    terms = notes[:, half_size : half_size + table_size].reshape(4 * positions, -1)
-    gain_total = jnp.sum(notes[:, half_size + table_size : size], axis=0).reshape(2, 3)
-    all_types = type_of.T.reshape(-1)
-    select = jnp.arange(type_count, dtype=jnp.int32)[:, None] == all_types[None, :]
-    grad_table = jnp.dot(select.astype(F32), terms, precision=lax.Precision.HIGHEST)
+    note = jnp.pad(table_part, ((0, 0), (0, 0), (0, 384 - own))).reshape(positions, 18, 128)
+    note = note.transpose(1, 0, 2).reshape(72, 128)
+    gain_row = jnp.pad(gain_sum.reshape(1, 6), ((0, 4), (0, 122)))
+    note = jnp.concatenate([half_sum, gain_row, note], axis=0).astype(BF16)
+    notes = lax.all_gather(note, LAT, axis=0)
     factor = 1.0 / math.sqrt(inputs.shape[0] * inputs.shape[1] * inputs.shape[2] * 4 * lons)
-    whole = whole * factor
-
-    def joined(at):
-        ends = whole[:, at + 6 : at + 9].reshape(2, 3, 2, 64).transpose(0, 2, 1, 3)
-        rows = jnp.concatenate([whole[:, at : at + 6], ends.reshape(2, 6, 64)], axis=2)
-        return rows.reshape(12, D)
-
-    grad_up = joined(0).T
-    rows = joined(18)
-    grad_qkv = rows[:9].T
-    grad_proj = rows[9:].T
-    grad_down = whole[:, 9:18].reshape(2, 3, 3, 128).transpose(0, 2, 1, 3).reshape(2, 3, lons, 6)
-    grad_down = grad_down.transpose(2, 0, 3, 1).reshape(FFN, 3)
-    return (
-        grad_input,
-        grad_qkv,
-        grad_proj,
-        grad_up,
-        grad_down,
-        gain_total * factor,
-        grad_table.reshape(type_count, HEADS, own),
-    )
+    shapes = [w.shape[::-1] for w in (qkv_weight, proj_weight, up_weight, down_weight)]
+    shapes += [norm_gains.shape, (HEADS, type_count, own)]
+    out = [(shape, F32) for shape in shapes]
+    kernel = functools.partial(finish_kernel, factor)
+    grads = small_call(kernel, (type_of, notes), 1, out, [], "finish")
+    table = grads[5].transpose(1, 0, 2)
+    return (grad_input, grads[0].T, grads[1].T, grads[2].T, grads[3].T, grads[4], table)
 
 
 def solution(mesh):

time: 119 us -> 115 us (0.966)
  local copies, waits for them, and re-layouts: 10.6 us -> 3.76 us
  Pallas kernels: 17.4 us -> 21.8 us
    pallas_call x0 -> x2, Pallas kernels: none -> 4.44 us  [small_call(): pl.pallas_call(kernel, in_specs=[flat] * scalars + [whole] * (len(args) -...]
    reshape x19 -> x1, local copies, waits for them, and re-layouts: 2.49 us -> 0.02 us  [shards(): jnp.pad(table_part, ((0, 0), (0, 0), (0, 384 - own)))]
    transpose x12 -> x1, local copies, waits for them, and re-layouts: 1.62 us -> 0.01 us  [shards(): note = note.transpose(1, 0, 2).reshape(72, 128)]
  transfers between devices with their start and end apart: 13 -> 13, of which waited for: 11 -> 11; matrix products, arithmetic and copies ran while one was open for 5% -> 4% of each run, Pallas kernels for 0% -> 2%
where the time goes in v2:
time: 115 us
  starting transfers between devices  41.3 us (36%)
  waiting for transfers between devices  27.7 us (24%)
  Pallas kernels  21.8 us (19%)
  blocking collectives  12.4 us (11%)
  other arithmetic  6.78 us (6%)
  local copies, waits for them, and re-layouts  3.76 us (3%)
    ppermute x11, starting transfers between devices, passed_along(): lax.ppermute(block, axes, [((i - distance) % size, i) for i in range(size)])  22.1 us
    ppermute x11, waiting for transfers between devices, passed_along(): lax.ppermute(block, axes, [((i - distance) % size, i) for i in range(size)])  21.9 us
    pallas_call x1, Pallas kernels, block_grads(): pl.pallas_call(block_kernel, in_specs=[pl.BlockSpec(memory_space=pltpu.SM...  17.4 us
    all_to_all x1, starting transfers between devices, shards(): landed = lax.all_to_all(parcel, LON, 0, 0)  12.4 us
    all_gather x1, blocking collectives, shards(): notes = lax.all_gather(note, LAT, axis=0)  9.74 us
    all_to_all x1, starting transfers between devices, shards(): returned = lax.all_to_all(parcel, LON, 0, 0)  6.78 us
    all_to_all x1, waiting for transfers between devices, shards(): landed = lax.all_to_all(parcel, LON, 0, 0)  4.56 us
    pallas_call x2, Pallas kernels, small_call(): pl.pallas_call(kernel, in_specs=[flat] * scalars + [whole] * (len(args) -...  4.44 us
  transfers between devices with their start and end apart: 13, of which 11 were waited for; matrix products, arithmetic and copies ran while one was open for 4% of the time, Pallas kernels for 2%

profile of v2, /device:TPU:1, one launch (start us, length us, event | category | flops | bytes accessed | tf_op | source)
XLA Modules:
  0.0 114.8 jit_solution(3878351896059287408)
XLA Ops:
  0.6 1.3 %slice_maximum_fusion = bf16[7,6,12,384]{3,0,2,1:T(8,128)(2,1)S(1)} fusion(bf16[8,6,12,192]{3,0,2,1:T(8,128)(2,1)} %param.11, bf16[8,6,12,192]{3,0,2,1:T(8,128)(2,1)} %param.10), kind=kLoop, calls=%fused_computation.12 | loop fusion | flops 774144 | bytes 829440 | tf_op jit(solution)/shard_map/concatenate | solution.py:490
  1.9 1.4 %fusion.3 = bf16[8,6,12,384]{3,0,2,1:T(8,128)(2,1)S(1)} fusion(bf16[8,6,12,192]{3,0,2,1:T(8,128)(2,1)} %param.11, bf16[8,6,12,192]{3,0,2,1:T(8,128)(2,1)} %param.10, bf16[7,6,12,384]{3,0,2,1:T(8,128)(2,1)S(1)} %slice_maximum_fusion), kind=kLoop, calls=%fused_computation.11 | loop fusion | flops 1327104 | bytes 1271808 | tf_op jit(solution)/shard_map/jit(_roll_static)/concatenate | solution.py:491
  3.8 0.6 fusion.5
  4.5 3.3 %collective-permute-start = (bf16[4,72,384]{2,1,0:T(8,128)(2,1)S(1)}, bf16[4,72,384]{2,1,0:T(8,128)(2,1)S(1)}, u32[]{:S(2)}, u32[]{:S(2)}) collective-permute-start(bf16[4,72,384]{2,1,0:T(8,128)(2,1)S(1)} %bitcast.99), channel_id=1, source_target_pairs={{64,0},{128,64},{192,128},{0,192},{65,1},{129,65},{193,129},{1,193... | collective-permute-start | bytes 663560 | tf_op jit(solution)/shard_map/ppermute | solution.py:27
  8.4 2.4 %pack.1 = bf16[64,48,128]{2,1,0:T(8,128)(2,1)} custom-call(s32[3]{0:T(128)} %pad_add_fusion.spot_ref, s32[4,4]{1,0:T(4,128)} %types_ref.3, bf16[9,192]{1,0:T(8,128)(2,1)} %bitcast.106, bf16[3,192]{1,0:T(4,128)(2,1)} %bitcast.109, bf16[12,192]{1,0:T(8,128)(2,1)} %bitcast.107, bf16[3,768]{1,0:T(4,128)(2,1)} %bitcast.108, bf16[2,3]{1,0:T(2,128)(2,1)} %gains_ref.1, ...), custom_call_target="tpu_custom_call" | custom-call | tf_op jit(solution)/shard_map/pack/pallas_call | solution.py:458
  10.8 1.7 %collective-permute-done = bf16[4,72,384]{2,1,0:T(8,128)(2,1)S(1)} collective-permute-done((bf16[4,72,384]{2,1,0:T(8,128)(2,1)S(1)}, bf16[4,72,384]{2,1,0:T(8,128)(2,1)S(1)}, u32[]{:S(2)}, u32[]{:S(2)}) %collective-permute-start) | collective-permute-done | bytes 221216 | tf_op jit(solution)/shard_map/ppermute | solution.py:27
  12.5 12.4 %all-to-all-start = ((bf16[64,48,128]{2,1,0:T(8,128)(2,1)}), bf16[64,48,128]{2,1,0:T(8,128)(2,1)S(1)}, u32[]{:S(2)}, u32[]{:S(2)}) async-start(bf16[64,48,128]{2,1,0:T(8,128)(2,1)} %pack.1), calls=%async_computation | async-start | bytes 1572864 | tf_op jit(solution)/shard_map/all_to_all | solution.py:507
  25.0 0.7 fusion.1
  25.7 1.1 collective-permute-start.1
  26.8 2.4 %collective-permute-start.2 = (bf16[144,384]{1,0:T(8,128)(2,1)S(1)}, bf16[144,384]{1,0:T(8,128)(2,1)S(1)}, u32[]{:S(2)}, u32[]{:S(2)}) collective-permute-start(bf16[144,384]{1,0:T(8,128)(2,1)S(1)} %get-tuple-element.38), channel_id=1, source_target_pairs={{2,0},{3,1},{0,2},{1,3},{6,4},{7,5},{4,6},{5,7},{10,8},{11,9},{8,1... | collective-permute-start | bytes 331784 | tf_op jit(solution)/shard_map/ppermute | solution.py:27
  29.2 1.2 %collective-permute-start.3 = (bf16[144,384]{1,0:T(8,128)(2,1)S(1)}, bf16[144,384]{1,0:T(8,128)(2,1)S(1)}, u32[]{:S(2)}, u32[]{:S(2)}) collective-permute-start(bf16[144,384]{1,0:T(8,128)(2,1)S(1)} %get-tuple-element.37), channel_id=1, source_target_pairs={{1,0},{2,1},{3,2},{0,3},{5,4},{6,5},{7,6},{4,7},{9,8},{10,9},{11,1... | collective-permute-start | bytes 331784 | tf_op jit(solution)/shard_map/ppermute | solution.py:27
  30.7 2.5 %collective-permute-done.1.b1 = bf16[144,384]{1,0:T(8,128)(2,1)S(1)} collective-permute-done((bf16[144,384]{1,0:T(8,128)(2,1)S(1)}, bf16[144,384]{1,0:T(8,128)(2,1)S(1)}, u32[]{:S(2)}, u32[]{:S(2)}) %collective-permute-start.1) | collective-permute-done | bytes 110624 | tf_op jit(solution)/shard_map/ppermute | solution.py:27
  33.2 5.0 %collective-permute-done.2.b2 = bf16[144,384]{1,0:T(8,128)(2,1)S(1)} collective-permute-done((bf16[144,384]{1,0:T(8,128)(2,1)S(1)}, bf16[144,384]{1,0:T(8,128)(2,1)S(1)}, u32[]{:S(2)}, u32[]{:S(2)}) %collective-permute-start.2) | collective-permute-done | bytes 110624 | tf_op jit(solution)/shard_map/ppermute | solution.py:27
  38.7 4.8 %collective-permute-start.4 = (bf16[144,384]{1,0:T(8,128)(2,1)S(1)}, bf16[144,384]{1,0:T(8,128)(2,1)S(1)}, u32[]{:S(2)}, u32[]{:S(2)}) collective-permute-start(bf16[144,384]{1,0:T(8,128)(2,1)S(1)} %select_select_fusion), channel_id=1, source_target_pairs={{4,0},{8,4},{12,8},{16,12},{20,16},{24,20},{28,24},{32,28},{36,32}... | collective-permute-start | bytes 331784 | tf_op jit(solution)/shard_map/ppermute | solution.py:27
  43.5 4.6 %all-to-all-done.landed_ref = bf16[64,48,128]{2,1,0:T(8,128)(2,1)S(1)} async-done(((bf16[64,48,128]{2,1,0:T(8,128)(2,1)}), bf16[64,48,128]{2,1,0:T(8,128)(2,1)S(1)}, u32[]{:S(2)}, u32[]{:S(2)}) %all-to-all-start) | async-done | bytes 786464 | tf_op jit(solution)/shard_map/all_to_all | solution.py:507
  48.3 2.6 %all-gather = bf16[128,27,128]{2,0,1:T(8,128)(2,1)S(1)} all-gather(bf16[64,27,128]{2,0,1:T(8,128)(2,1)S(1)} %copy.57), channel_id=2, replica_groups=mesh['yh'=2,'core'=2,'yl'=2,'z'=8,'x'=4] {'core'}, dimensions={0}, use_global_device_ids=true | all-gather | bytes 1327104 | tf_op jit(solution)/shard_map/all_gather | solution.py:514
  50.9 0.6 copy.58
  51.5 17.4 %block_grads.1 = (bf16[4,144,192]{2,1,0:T(8,128)(2,1)S(1)}, bf16[144,192]{1,0:T(8,128)(2,1)S(1)}, bf16[64,27,128]{2,1,0:T(8,128)(2,1)S(1)}, bf16[64,27,128]{2,1,0:T(8,128)(2,1)S(1)}, bf16[64,21,128]{2,1,0:T(8,128)(2,1)S(1)}) custom-call(s32[1]{0:T(128)} %bitcast.last_ref, s32[1]{0:T(128)} %bitcast.1.core_ref, bf16[144,384]{1,0:T(8,128)(2,1)S(1)} %get-tuple-element.40.b0, ...), custom_call_target="tpu_custom_call" | custom-call | tf_op jit(solution)/shard_map/block_grads/pallas_call | solution.py:346
  69.1 1.8 %collective-permute-done.5 = bf16[64,27,128]{2,1,0:T(8,128)(2,1)S(1)} collective-permute-done((bf16[64,27,128]{2,1,0:T(8,128)(2,1)S(1)}, bf16[64,27,128]{2,1,0:T(8,128)(2,1)S(1)}, u32[]{:S(2)}, u32[]{:S(2)}) %collective-permute-start.5) | collective-permute-done | bytes 442400 | tf_op jit(solution)/shard_map/ppermute | solution.py:27
  71.1 1.1 pad_maximum_fusion
  72.2 1.4 %collective-permute-start.6 = (bf16[144,192]{1,0:T(8,128)(2,1)S(1)}, bf16[144,192]{1,0:T(8,128)(2,1)S(1)}, u32[]{:S(2)}, u32[]{:S(2)}) collective-permute-start(bf16[144,192]{1,0:T(8,128)(2,1)S(1)} %get-tuple-element.29), channel_id=1, source_target_pairs={{60,0},{0,4},{4,8},{8,12},{12,16},{16,20},{20,24},{24,28},{28,32},... | collective-permute-start | bytes 165896 | tf_op jit(solution)/shard_map/ppermute | solution.py:27
  73.6 6.8 %all-to-all-start.1 = ((bf16[64,48,128]{2,1,0:T(8,128)(2,1)}), bf16[64,48,128]{2,1,0:T(8,128)(2,1)S(1)}, u32[]{:S(2)}, u32[]{:S(2)}) async-start(bf16[64,48,128]{2,1,0:T(8,128)(2,1)} %pad_maximum_fusion), calls=%async_computation.1 | async-start | bytes 1572864 | tf_op jit(solution)/shard_map/all_to_all | solution.py:526
  80.4 2.3 %collective-permute-start.7 = (bf16[144,192]{1,0:T(8,128)(2,1)S(1)}, bf16[144,192]{1,0:T(8,128)(2,1)S(1)}, u32[]{:S(2)}, u32[]{:S(2)}) collective-permute-start(bf16[144,192]{1,0:T(8,128)(2,1)S(1)} %get-tuple-element.45), channel_id=1, source_target_pairs={{1,0},{2,1},{3,2},{0,3},{5,4},{6,5},{7,6},{4,7},{9,8},{10,9},{11,1... | collective-permute-start | bytes 165896 | tf_op jit(solution)/shard_map/ppermute | solution.py:27
  83.9 0.7 collective-permute-done.7
  84.6 3.6 %collective-permute-done.8 = bf16[144,192]{1,0:T(8,128)(2,1)S(1)} collective-permute-done((bf16[144,192]{1,0:T(8,128)(2,1)S(1)}, bf16[144,192]{1,0:T(8,128)(2,1)S(1)}, u32[]{:S(2)}, u32[]{:S(2)}) %collective-permute-start.8) | collective-permute-done | bytes 55328 | tf_op jit(solution)/shard_map/ppermute | solution.py:27
  88.2 2.4 %collective-permute-done.9 = bf16[144,192]{1,0:T(8,128)(2,1)S(1)} collective-permute-done((bf16[144,192]{1,0:T(8,128)(2,1)S(1)}, bf16[144,192]{1,0:T(8,128)(2,1)S(1)}, u32[]{:S(2)}, u32[]{:S(2)}) %collective-permute-start.9) | collective-permute-done | bytes 55328 | tf_op jit(solution)/shard_map/ppermute | solution.py:27
  90.7 4.2 %collective-permute-start.10 = (bf16[4,72,192]{2,1,0:T(8,128)(2,1)S(1)}, bf16[4,72,192]{2,1,0:T(8,128)(2,1)S(1)}, u32[]{:S(2)}, u32[]{:S(2)}) collective-permute-start(bf16[4,72,192]{2,1,0:T(8,128)(2,1)S(1)} %get-tuple-element.46), channel_id=1, source_target_pairs={{192,0},{0,64},{64,128},{128,192},{193,1},{1,65},{65,129},{129,193... | collective-permute-start | bytes 331784 | tf_op jit(solution)/shard_map/ppermute | solution.py:27
  94.9 3.8 %collective-permute-done.10 = bf16[4,72,192]{2,1,0:T(8,128)(2,1)S(1)} collective-permute-done((bf16[4,72,192]{2,1,0:T(8,128)(2,1)S(1)}, bf16[4,72,192]{2,1,0:T(8,128)(2,1)S(1)}, u32[]{:S(2)}, u32[]{:S(2)}) %collective-permute-start.10) | collective-permute-done | bytes 110624 | tf_op jit(solution)/shard_map/ppermute | solution.py:27
  99.6 0.9 pad_maximum_fusion.2
  100.5 1.3 %all-to-all-done.1 = bf16[64,48,128]{2,1,0:T(8,128)(2,1)S(1)} async-done(((bf16[64,48,128]{2,1,0:T(8,128)(2,1)}), bf16[64,48,128]{2,1,0:T(8,128)(2,1)S(1)}, u32[]{:S(2)}, u32[]{:S(2)}) %all-to-all-start.1) | async-done | bytes 786464 | tf_op jit(solution)/shard_map/all_to_all | solution.py:526
  103.0 9.7 %all_gather.12.notes_ref = bf16[4,104,128]{2,1,0:T(8,128)(2,1)} all-gather(bf16[1,104,128]{2,1,0:T(8,128)(2,1)S(1)} %pad_maximum_fusion.4), channel_id=1, replica_groups=mesh['yh'=2,'core'=2,'yl'=2,'z'=8,'x'=4] {'yh','core'}, dimensions={0}, use_global_device_ids=true | all-gather | bytes 133120 | tf_op jit(solution)/shard_map/all_gather | solution.py:550
  112.7 2.1 %finish.1 = (f32[9,192]{1,0:T(8,128)}, f32[3,192]{1,0:T(4,128)}, f32[12,192]{1,0:T(8,128)}, f32[3,768]{1,0:T(4,128)}, f32[2,3]{1,0:T(2,128)}, /*index=5*/f32[6,16,324]{2,1,0:T(8,128)}) custom-call(s32[4,4]{1,0:T(4,128)} %types_ref.3, bf16[4,104,128]{2,1,0:T(8,128)(2,1)} %all_gather.12.notes_ref), custom_call_target="tpu_custom_call" | custom-call | tf_op jit(solution)/shard_map/finish/pallas_call | solution.py:458
  (60 shorter events, 5.8 us)
Async XLA Ops:
  0.6 29.8 %copy-start = (s32[8,6]{1,0:T(8,128)S(1)}, s32[8,6]{1,0:T(8,128)}, u32[]{:S(2)}) copy-start(s32[8,6]{1,0:T(8,128)} %param.19) | copy-start | bytes 580
  4.5 8.0 %collective-permute-start = (bf16[4,72,384]{2,1,0:T(8,128)(2,1)S(1)}, bf16[4,72,384]{2,1,0:T(8,128)(2,1)S(1)}, u32[]{:S(2)}, u32[]{:S(2)}) collective-permute-start(bf16[4,72,384]{2,1,0:T(8,128)(2,1)S(1)} %bitcast.99), channel_id=1, source_target_pairs={{64,0},{128,64},{192,128},{0,192},{65,1},{129,65},{193,129},{1,193... | collective-permute-start | bytes 663560 | tf_op jit(solution)/shard_map/ppermute | solution.py:27
  12.5 35.6 %all-to-all-start = ((bf16[64,48,128]{2,1,0:T(8,128)(2,1)}), bf16[64,48,128]{2,1,0:T(8,128)(2,1)S(1)}, u32[]{:S(2)}, u32[]{:S(2)}) async-start(bf16[64,48,128]{2,1,0:T(8,128)(2,1)} %pack.1), calls=%async_computation | async-start | bytes 1572864 | tf_op jit(solution)/shard_map/all_to_all | solution.py:507
  25.7 7.5 %collective-permute-start.1 = (bf16[144,384]{1,0:T(8,128)(2,1)S(1)}, bf16[144,384]{1,0:T(8,128)(2,1)S(1)}, u32[]{:S(2)}, u32[]{:S(2)}) collective-permute-start(bf16[144,384]{1,0:T(8,128)(2,1)S(1)} %get-tuple-element.39), channel_id=1, source_target_pairs={{3,0},{0,1},{1,2},{2,3},{7,4},{4,5},{5,6},{6,7},{11,8},{8,9},{9,10... | collective-permute-start | bytes 331784 | tf_op jit(solution)/shard_map/ppermute | solution.py:27
  26.8 11.4 %collective-permute-start.2 = (bf16[144,384]{1,0:T(8,128)(2,1)S(1)}, bf16[144,384]{1,0:T(8,128)(2,1)S(1)}, u32[]{:S(2)}, u32[]{:S(2)}) collective-permute-start(bf16[144,384]{1,0:T(8,128)(2,1)S(1)} %get-tuple-element.38), channel_id=1, source_target_pairs={{2,0},{3,1},{0,2},{1,3},{6,4},{7,5},{4,6},{5,7},{10,8},{11,9},{8,1... | collective-permute-start | bytes 331784 | tf_op jit(solution)/shard_map/ppermute | solution.py:27
  29.2 9.4 %collective-permute-start.3 = (bf16[144,384]{1,0:T(8,128)(2,1)S(1)}, bf16[144,384]{1,0:T(8,128)(2,1)S(1)}, u32[]{:S(2)}, u32[]{:S(2)}) collective-permute-start(bf16[144,384]{1,0:T(8,128)(2,1)S(1)} %get-tuple-element.37), channel_id=1, source_target_pairs={{1,0},{2,1},{3,2},{0,3},{5,4},{6,5},{7,6},{4,7},{9,8},{10,9},{11,1... | collective-permute-start | bytes 331784 | tf_op jit(solution)/shard_map/ppermute | solution.py:27
  38.7 12.8 %collective-permute-start.4 = (bf16[144,384]{1,0:T(8,128)(2,1)S(1)}, bf16[144,384]{1,0:T(8,128)(2,1)S(1)}, u32[]{:S(2)}, u32[]{:S(2)}) collective-permute-start(bf16[144,384]{1,0:T(8,128)(2,1)S(1)} %select_select_fusion), channel_id=1, source_target_pairs={{4,0},{8,4},{12,8},{16,12},{20,16},{24,20},{28,24},{32,28},{36,32}... | collective-permute-start | bytes 331784 | tf_op jit(solution)/shard_map/ppermute | solution.py:27
  68.9 2.0 %collective-permute-start.5 = (bf16[64,27,128]{2,1,0:T(8,128)(2,1)S(1)}, bf16[64,27,128]{2,1,0:T(8,128)(2,1)S(1)}, u32[]{:S(2)}, u32[]{:S(2)}) collective-permute-start(bf16[64,27,128]{2,1,0:T(8,128)(2,1)S(1)} %get-tuple-element.26), channel_id=1, source_target_pairs={{64,0},{0,64},{65,1},{1,65},{66,2},{2,66},{67,3},{3,67},{68,4},{4,... | collective-permute-start | bytes 1327112 | tf_op jit(solution)/shard_map/ppermute | solution.py:27
  72.2 8.2 %collective-permute-start.6 = (bf16[144,192]{1,0:T(8,128)(2,1)S(1)}, bf16[144,192]{1,0:T(8,128)(2,1)S(1)}, u32[]{:S(2)}, u32[]{:S(2)}) collective-permute-start(bf16[144,192]{1,0:T(8,128)(2,1)S(1)} %get-tuple-element.29), channel_id=1, source_target_pairs={{60,0},{0,4},{4,8},{8,12},{12,16},{16,20},{20,24},{24,28},{28,32},... | collective-permute-start | bytes 165896 | tf_op jit(solution)/shard_map/ppermute | solution.py:27
  73.6 28.2 %all-to-all-start.1 = ((bf16[64,48,128]{2,1,0:T(8,128)(2,1)}), bf16[64,48,128]{2,1,0:T(8,128)(2,1)S(1)}, u32[]{:S(2)}, u32[]{:S(2)}) async-start(bf16[64,48,128]{2,1,0:T(8,128)(2,1)} %pad_maximum_fusion), calls=%async_computation.1 | async-start | bytes 1572864 | tf_op jit(solution)/shard_map/all_to_all | solution.py:526
  80.4 4.1 %collective-permute-start.7 = (bf16[144,192]{1,0:T(8,128)(2,1)S(1)}, bf16[144,192]{1,0:T(8,128)(2,1)S(1)}, u32[]{:S(2)}, u32[]{:S(2)}) collective-permute-start(bf16[144,192]{1,0:T(8,128)(2,1)S(1)} %get-tuple-element.45), channel_id=1, source_target_pairs={{1,0},{2,1},{3,2},{0,3},{5,4},{6,5},{7,6},{4,7},{9,8},{10,9},{11,1... | collective-permute-start | bytes 165896 | tf_op jit(solution)/shard_map/ppermute | solution.py:27
  82.7 5.4 %collective-permute-start.8 = (bf16[144,192]{1,0:T(8,128)(2,1)S(1)}, bf16[144,192]{1,0:T(8,128)(2,1)S(1)}, u32[]{:S(2)}, u32[]{:S(2)}) collective-permute-start(bf16[144,192]{1,0:T(8,128)(2,1)S(1)} %get-tuple-element.44), channel_id=1, source_target_pairs={{2,0},{3,1},{0,2},{1,3},{6,4},{7,5},{4,6},{5,7},{10,8},{11,9},{8,1... | collective-permute-start | bytes 165896 | tf_op jit(solution)/shard_map/ppermute | solution.py:27
  83.3 7.2 %collective-permute-start.9 = (bf16[144,192]{1,0:T(8,128)(2,1)S(1)}, bf16[144,192]{1,0:T(8,128)(2,1)S(1)}, u32[]{:S(2)}, u32[]{:S(2)}) collective-permute-start(bf16[144,192]{1,0:T(8,128)(2,1)S(1)} %get-tuple-element.43), channel_id=1, source_target_pairs={{3,0},{0,1},{1,2},{2,3},{7,4},{4,5},{5,6},{6,7},{11,8},{8,9},{9,10... | collective-permute-start | bytes 165896 | tf_op jit(solution)/shard_map/ppermute | solution.py:27
  90.7 8.0 %collective-permute-start.10 = (bf16[4,72,192]{2,1,0:T(8,128)(2,1)S(1)}, bf16[4,72,192]{2,1,0:T(8,128)(2,1)S(1)}, u32[]{:S(2)}, u32[]{:S(2)}) collective-permute-start(bf16[4,72,192]{2,1,0:T(8,128)(2,1)S(1)} %get-tuple-element.46), channel_id=1, source_target_pairs={{192,0},{0,64},{64,128},{128,192},{193,1},{1,65},{65,129},{129,193... | collective-permute-start | bytes 331784 | tf_op jit(solution)/shard_map/ppermute | solution.py:27

commit v3 on v2

--- a/solution.py
+++ b/solution.py
@@ -69,12 +69,16 @@
     return jnp.concatenate([rows[:36], rows[72:108], rows[36:72], rows[108:]], axis=0)
 
 
-def unpack_weights(halves_ref, qkv_ref, proj_ref, up_ref, down_ref):
+def unpack_weights(core, mine_ref, other_ref, qkv_ref, proj_ref, up_ref, down_ref):
     def stack(pieces):
         return jnp.concatenate(pieces, axis=0).astype(BF16)
 
     for g in range(4):
-        v = [[halves_ref[c, 16 * g + i].astype(F32) for i in range(16)] for c in range(2)]
+        mine = [mine_ref[16 * g + i, :32, :].astype(F32)[:27] for i in range(16)]
+        other = [other_ref[16 * g + i, :32, :].astype(F32)[:27] for i in range(16)]
+        v = [
+            [jnp.where(core == c, a, b) for a, b in zip(mine, other)] for c in range(2)
+        ]
         for c in range(2):
             rows = slice(c * 384 + 96 * g, c * 384 + 96 * (g + 1))
             up_ref[rows, :128] = stack([p[:6] for p in v[c]])
@@ -170,7 +174,7 @@
     place = lax.broadcasted_iota(jnp.int32, (WIN, 1), 0) % WLON
     is_left = place < WLON // 2
     same = row_label_ref[...] == col_label_ref[...]
-    unpack_weights(halves_ref, qkv_ref, proj_ref, up_ref, down_ref)
+    unpack_weights(core_ref[0], landed_ref, halves_ref, qkv_ref, proj_ref, up_ref, down_ref)
     source = lax.broadcasted_iota(jnp.int32, (WIN, 192), 1)
     target = lax.broadcasted_iota(jnp.int32, (WIN, 192), 0)
     held = 9 * (source // 12) + 2 * (source // 3 % 4) + source % 3
@@ -487,10 +491,12 @@
     members = lax.axis_size("x")
     lons = groups * members
 
-    cells = jnp.concatenate([inputs, cotangent], axis=-1)
-    cells = jnp.roll(cells, -1, axis=0).reshape(positions, WPL, 2, WLAT // 2, WLON, 2 * D)
-    cells = cells.transpose(0, 2, 1, 3, 4, 5).reshape(positions, 2, WIN // 2, 2 * D)
-
+    def side_by_side(one, two):
+        both = jnp.roll(jnp.concatenate([one, two], axis=-1), -1, axis=0)
+        return both.reshape(positions, WIN // 2, 2 * D)
+
+    rows = WLAT // 2
+    arrived = [passed_along(a[:, :rows], LAT, -1) for a in (inputs, cotangent)]
     spot = jnp.stack([x_index, core, lat_index]).astype(jnp.int32)
     weights = [w.T for w in (qkv_weight, proj_weight, up_weight, down_weight)]
     weights += [norm_gains, bias_table.transpose(1, 0, 2)]
@@ -498,9 +504,9 @@
         pack_kernel, (spot, type_of, *weights), 2, [((lons, 48, 128), BF16)], [], "pack"
     )
 
-    arrived = passed_along(cells[:, 0], LAT, -1)
     parcel, arrived = lax.optimization_barrier((parcel, arrived))
-    cells = jnp.concatenate([cells[:, 1], arrived], axis=1)
+    cells = side_by_side(inputs[:, rows:], cotangent[:, rows:])
+    cells = jnp.concatenate([cells, side_by_side(*arrived)], axis=1)
     cells = jnp.concatenate([cells, cells[: members - 1]], axis=0)
     cells = lax.dynamic_slice_in_dim(cells, x_index, members, 0)
     blocks = [cells[0]] + [passed_along(cells[k], ("x",), k) for k in range(1, members)]
@@ -510,8 +516,9 @@
     for k in range(1, members):
         rim = jnp.where(is_first[k], blocks[k], rim)
     rim = passed_along(rim, ("yl", "z"), -1)
+    landed, rim = lax.optimization_barrier((landed, rim))
     last = (x_index + 1) % members
-    halves = lax.all_gather(landed[:, :27], "core", axis=0)
+    halves = passed_along(landed, ("core",), 1)
 
     labels = lax.dynamic_slice(region, (x_index * WPL, jnp.int32(0)), (WPL, WLAT))
     labels = jnp.broadcast_to(labels[:, :, None], (WPL, WLAT, WLON)).reshape(WIN)

time: 115 us -> 112 us (0.974)
  waiting for transfers between devices: 27.7 us -> 31.6 us
  blocking collectives: 12.4 us -> 9.61 us
  other arithmetic: 6.78 us -> 4.19 us
    ppermute x11 -> x13, waiting for transfers between devices: 21.9 us -> 27.5 us  [passed_along(): lax.ppermute(block, axes, [((i - distance) % size, i) for i in range(size)])]
    all_gather x1 -> x0, blocking collectives: 2.62 us -> none  [shards(): halves = lax.all_gather(landed[:, :27], 'core', axis=0)]
    all_to_all x1, waiting for transfers between devices: 4.56 us -> 2.06 us  [shards(): landed = lax.all_to_all(parcel, LON, 0, 0)]
    concatenate x2 -> x4, other arithmetic: 2.64 us -> 0.57 us  [side_by_side(): both = jnp.roll(jnp.concatenate([one, two], axis=-1), -1, axis=0)]
    ppermute x11 -> x13, starting transfers between devices: 22.1 us -> 21.6 us  [passed_along(): lax.ppermute(block, axes, [((i - distance) % size, i) for i in range(size)])]
  transfers between devices with their start and end apart: 13 -> 15, of which waited for: 11 -> 12; matrix products, arithmetic and copies ran while one was open for 4% -> 4% of each run, Pallas kernels for 2% -> 2%
where the time goes in v3:
time: 112 us
  starting transfers between devices  40.2 us (36%)
  waiting for transfers between devices  31.6 us (28%)
  Pallas kernels  21.9 us (20%)
  blocking collectives  9.61 us (9%)
  other arithmetic  4.19 us (4%)
  local copies, waits for them, and re-layouts  3.21 us (3%)
    ppermute x13, waiting for transfers between devices, passed_along(): lax.ppermute(block, axes, [((i - distance) % size, i) for i in range(size)])  27.5 us
    ppermute x13, starting transfers between devices, passed_along(): lax.ppermute(block, axes, [((i - distance) % size, i) for i in range(size)])  21.6 us
    pallas_call x1, Pallas kernels, block_grads(): pl.pallas_call(block_kernel, in_specs=[pl.BlockSpec(memory_space=pltpu.SM...  17.4 us
    all_to_all x1, starting transfers between devices, shards(): landed = lax.all_to_all(parcel, LON, 0, 0)  11.8 us
    all_gather x1, blocking collectives, shards(): notes = lax.all_gather(note, LAT, axis=0)  9.61 us
    all_to_all x1, starting transfers between devices, shards(): returned = lax.all_to_all(parcel, LON, 0, 0)  6.78 us
    pallas_call x2, Pallas kernels, small_call(): pl.pallas_call(kernel, in_specs=[flat] * scalars + [whole] * (len(args) -...  4.45 us
  transfers between devices with their start and end apart: 15, of which 12 were waited for; matrix products, arithmetic and copies ran while one was open for 4% of the time, Pallas kernels for 2%

profile of v3, /device:TPU:1, one launch (start us, length us, event | category | flops | bytes accessed | tf_op | source)
XLA Modules:
  0.0 111.7 jit_solution(61369827045560160)
XLA Ops:
  0.6 1.2 %fusion.4 = (bf16[8,3,12,192]{3,0,2,1:T(8,128)(2,1)S(1)}, bf16[8,3,12,192]{3,0,2,1:T(8,128)(2,1)S(1)}, bf16[8,3,12,192]{3,0,2,1:T(8,128)(2,1)S(1)}, bf16[8,3,12,192]{3,0,2,1:T(8,128)(2,1)S(1)}) fusion(bf16[8,6,12,192]{3,0,2,1:T(8,128)(2,1)} %param.11, bf16[8,6,12,192]{3,0,2,1:T(8,128)(2,1)} %param.10), kind=kLoop, calls=%fused_computation.45 | loop fusion | bytes 884736 | tf_op jit(solution)/shard_map/slice | solution.py:499
  1.8 3.3 %collective-permute-start = (bf16[8,3,12,192]{3,0,2,1:T(8,128)(2,1)S(1)}, bf16[8,3,12,192]{3,0,2,1:T(8,128)(2,1)S(1)}, u32[]{:S(2)}, u32[]{:S(2)}) collective-permute-start(bf16[8,3,12,192]{3,0,2,1:T(8,128)(2,1)S(1)} %get-tuple-element.57), channel_id=1, source_target_pairs={{64,0},{128,64},{192,128},{0,192},{65,1},{129,65},{193,129},{1,193... | collective-permute-start | bytes 331784 | tf_op jit(solution)/shard_map/ppermute | solution.py:27
  5.1 0.9 collective-permute-start.1
  6.0 0.6 pad_add_fusion.spot_ref
  6.6 2.4 %pack.1 = bf16[64,48,128]{2,1,0:T(8,128)(2,1)} custom-call(s32[3]{0:T(128)} %pad_add_fusion.spot_ref, s32[4,4]{1,0:T(4,128)} %types_ref.3, bf16[9,192]{1,0:T(8,128)(2,1)} %bitcast.88, bf16[3,192]{1,0:T(4,128)(2,1)} %bitcast.91, bf16[12,192]{1,0:T(8,128)(2,1)} %bitcast.89, bf16[3,768]{1,0:T(4,128)(2,1)} %bitcast.90, bf16[2,3]{1,0:T(2,128)(2,1)} %gains_ref.1, ...), custom_call_target="tpu_custom_call" | custom-call | tf_op jit(solution)/shard_map/pack/pallas_call | solution.py:462
  9.0 2.2 %collective-permute-done.1 = bf16[8,3,12,192]{3,0,2,1:T(8,128)(2,1)S(1)} collective-permute-done((bf16[8,3,12,192]{3,0,2,1:T(8,128)(2,1)S(1)}, bf16[8,3,12,192]{3,0,2,1:T(8,128)(2,1)S(1)}, u32[]{:S(2)}, u32[]{:S(2)}) %collective-permute-start.1) | collective-permute-done | bytes 110624 | tf_op jit(solution)/shard_map/ppermute | solution.py:27
  11.2 11.8 %all-to-all-start = ((bf16[64,48,128]{2,1,0:T(8,128)(2,1)}), bf16[64,48,128]{2,1,0:T(8,128)(2,1)S(1)}, u32[]{:S(2)}, u32[]{:S(2)}) async-start(bf16[64,48,128]{2,1,0:T(8,128)(2,1)} %pack.1), calls=%async_computation | async-start | bytes 1572864 | tf_op jit(solution)/shard_map/all_to_all | solution.py:513
  24.2 1.1 collective-permute-start.2
  25.3 2.4 %collective-permute-start.3 = (bf16[144,384]{1,0:T(8,128)(2,1)S(1)}, bf16[144,384]{1,0:T(8,128)(2,1)S(1)}, u32[]{:S(2)}, u32[]{:S(2)}) collective-permute-start(bf16[144,384]{1,0:T(8,128)(2,1)S(1)} %get-tuple-element.44), channel_id=1, source_target_pairs={{2,0},{3,1},{0,2},{1,3},{6,4},{7,5},{4,6},{5,7},{10,8},{11,9},{8,1... | collective-permute-start | bytes 331784 | tf_op jit(solution)/shard_map/ppermute | solution.py:27
  27.7 1.2 %collective-permute-start.4 = (bf16[144,384]{1,0:T(8,128)(2,1)S(1)}, bf16[144,384]{1,0:T(8,128)(2,1)S(1)}, u32[]{:S(2)}, u32[]{:S(2)}) collective-permute-start(bf16[144,384]{1,0:T(8,128)(2,1)S(1)} %get-tuple-element.43), channel_id=1, source_target_pairs={{1,0},{2,1},{3,2},{0,3},{5,4},{6,5},{7,6},{4,7},{9,8},{10,9},{11,1... | collective-permute-start | bytes 331784 | tf_op jit(solution)/shard_map/ppermute | solution.py:27
  28.9 2.8 %collective-permute-done.2.b1 = bf16[144,384]{1,0:T(8,128)(2,1)S(1)} collective-permute-done((bf16[144,384]{1,0:T(8,128)(2,1)S(1)}, bf16[144,384]{1,0:T(8,128)(2,1)S(1)}, u32[]{:S(2)}, u32[]{:S(2)}) %collective-permute-start.2) | collective-permute-done | bytes 110624 | tf_op jit(solution)/shard_map/ppermute | solution.py:27
  31.7 5.5 %collective-permute-done.3.b2 = bf16[144,384]{1,0:T(8,128)(2,1)S(1)} collective-permute-done((bf16[144,384]{1,0:T(8,128)(2,1)S(1)}, bf16[144,384]{1,0:T(8,128)(2,1)S(1)}, u32[]{:S(2)}, u32[]{:S(2)}) %collective-permute-start.3) | collective-permute-done | bytes 110624 | tf_op jit(solution)/shard_map/ppermute | solution.py:27
  37.2 4.8 %collective-permute-start.5 = (bf16[144,384]{1,0:T(8,128)(2,1)S(1)}, bf16[144,384]{1,0:T(8,128)(2,1)S(1)}, u32[]{:S(2)}, u32[]{:S(2)}) collective-permute-start(bf16[144,384]{1,0:T(8,128)(2,1)S(1)} %select_select_fusion), channel_id=1, source_target_pairs={{4,0},{8,4},{12,8},{16,12},{20,16},{24,20},{28,24},{32,28},{36,32}... | collective-permute-start | bytes 331784 | tf_op jit(solution)/shard_map/ppermute | solution.py:27
  42.1 2.1 %collective-permute-done.5.rim_ref = bf16[144,384]{1,0:T(8,128)(2,1)S(1)} collective-permute-done((bf16[144,384]{1,0:T(8,128)(2,1)S(1)}, bf16[144,384]{1,0:T(8,128)(2,1)S(1)}, u32[]{:S(2)}, u32[]{:S(2)}) %collective-permute-start.5) | collective-permute-done | bytes 110624 | tf_op jit(solution)/shard_map/ppermute | solution.py:27
  44.2 2.1 %all-to-all-done.landed_ref = bf16[64,48,128]{2,1,0:T(8,128)(2,1)S(1)} async-done(((bf16[64,48,128]{2,1,0:T(8,128)(2,1)}), bf16[64,48,128]{2,1,0:T(8,128)(2,1)S(1)}, u32[]{:S(2)}, u32[]{:S(2)}) %all-to-all-start) | async-done | bytes 786464 | tf_op jit(solution)/shard_map/all_to_all | solution.py:513
  46.5 2.0 %collective-permute-done.6.halves_ref = bf16[64,48,128]{2,1,0:T(8,128)(2,1)S(1)} collective-permute-done((bf16[64,48,128]{2,1,0:T(8,128)(2,1)S(1)}, bf16[64,48,128]{2,1,0:T(8,128)(2,1)S(1)}, u32[]{:S(2)}, u32[]{:S(2)}) %collective-permute-start.6) | collective-permute-done | bytes 786464 | tf_op jit(solution)/shard_map/ppermute | solution.py:27
  48.5 17.4 %block_grads.1 = (bf16[4,144,192]{2,1,0:T(8,128)(2,1)S(1)}, bf16[144,192]{1,0:T(8,128)(2,1)S(1)}, bf16[64,27,128]{2,1,0:T(8,128)(2,1)S(1)}, bf16[64,27,128]{2,1,0:T(8,128)(2,1)S(1)}, bf16[64,21,128]{2,1,0:T(8,128)(2,1)S(1)}) custom-call(s32[1]{0:T(128)} %bitcast.last_ref, s32[1]{0:T(128)} %bitcast.1.core_ref, bf16[144,384]{1,0:T(8,128)(2,1)S(1)} %get-tuple-element.46.b0, ...), custom_call_target="tpu_custom_call" | custom-call | tf_op jit(solution)/shard_map/block_grads/pallas_call | solution.py:350
  66.2 1.8 %collective-permute-done.7 = bf16[64,27,128]{2,1,0:T(8,128)(2,1)S(1)} collective-permute-done((bf16[64,27,128]{2,1,0:T(8,128)(2,1)S(1)}, bf16[64,27,128]{2,1,0:T(8,128)(2,1)S(1)}, u32[]{:S(2)}, u32[]{:S(2)}) %collective-permute-start.7) | collective-permute-done | bytes 442400 | tf_op jit(solution)/shard_map/ppermute | solution.py:27
  68.1 1.1 pad_maximum_fusion
  69.2 1.4 %collective-permute-start.8 = (bf16[144,192]{1,0:T(8,128)(2,1)S(1)}, bf16[144,192]{1,0:T(8,128)(2,1)S(1)}, u32[]{:S(2)}, u32[]{:S(2)}) collective-permute-start(bf16[144,192]{1,0:T(8,128)(2,1)S(1)} %get-tuple-element.35), channel_id=1, source_target_pairs={{60,0},{0,4},{4,8},{8,12},{12,16},{16,20},{20,24},{24,28},{28,32},... | collective-permute-start | bytes 165896 | tf_op jit(solution)/shard_map/ppermute | solution.py:27
  70.6 6.8 %all-to-all-start.1 = ((bf16[64,48,128]{2,1,0:T(8,128)(2,1)}), bf16[64,48,128]{2,1,0:T(8,128)(2,1)S(1)}, u32[]{:S(2)}, u32[]{:S(2)}) async-start(bf16[64,48,128]{2,1,0:T(8,128)(2,1)} %pad_maximum_fusion), calls=%async_computation.1 | async-start | bytes 1572864 | tf_op jit(solution)/shard_map/all_to_all | solution.py:533
  77.5 2.3 %collective-permute-start.9 = (bf16[144,192]{1,0:T(8,128)(2,1)S(1)}, bf16[144,192]{1,0:T(8,128)(2,1)S(1)}, u32[]{:S(2)}, u32[]{:S(2)}) collective-permute-start(bf16[144,192]{1,0:T(8,128)(2,1)S(1)} %get-tuple-element.49), channel_id=1, source_target_pairs={{1,0},{2,1},{3,2},{0,3},{5,4},{6,5},{7,6},{4,7},{9,8},{10,9},{11,1... | collective-permute-start | bytes 165896 | tf_op jit(solution)/shard_map/ppermute | solution.py:27
  79.8 0.6 collective-permute-start.10
  80.3 0.6 collective-permute-start.11
  81.4 4.1 %collective-permute-done.10 = bf16[144,192]{1,0:T(8,128)(2,1)S(1)} collective-permute-done((bf16[144,192]{1,0:T(8,128)(2,1)S(1)}, bf16[144,192]{1,0:T(8,128)(2,1)S(1)}, u32[]{:S(2)}, u32[]{:S(2)}) %collective-permute-start.10) | collective-permute-done | bytes 55328 | tf_op jit(solution)/shard_map/ppermute | solution.py:27
  85.4 3.2 %collective-permute-done.11 = bf16[144,192]{1,0:T(8,128)(2,1)S(1)} collective-permute-done((bf16[144,192]{1,0:T(8,128)(2,1)S(1)}, bf16[144,192]{1,0:T(8,128)(2,1)S(1)}, u32[]{:S(2)}, u32[]{:S(2)}) %collective-permute-start.11) | collective-permute-done | bytes 55328 | tf_op jit(solution)/shard_map/ppermute | solution.py:27
  88.8 2.8 %collective-permute-start.12 = (bf16[4,72,192]{2,1,0:T(8,128)(2,1)S(1)}, bf16[4,72,192]{2,1,0:T(8,128)(2,1)S(1)}, u32[]{:S(2)}, u32[]{:S(2)}) collective-permute-start(bf16[4,72,192]{2,1,0:T(8,128)(2,1)S(1)} %get-tuple-element.50), channel_id=1, source_target_pairs={{192,0},{0,64},{64,128},{128,192},{193,1},{1,65},{65,129},{129,193... | collective-permute-start | bytes 331784 | tf_op jit(solution)/shard_map/ppermute | solution.py:27
  91.6 3.5 %collective-permute-done.12 = bf16[4,72,192]{2,1,0:T(8,128)(2,1)S(1)} collective-permute-done((bf16[4,72,192]{2,1,0:T(8,128)(2,1)S(1)}, bf16[4,72,192]{2,1,0:T(8,128)(2,1)S(1)}, u32[]{:S(2)}, u32[]{:S(2)}) %collective-permute-start.12) | collective-permute-done | bytes 110624 | tf_op jit(solution)/shard_map/ppermute | solution.py:27
  96.0 0.9 pad_maximum_fusion.1
  96.9 2.0 %all-to-all-done.1 = bf16[64,48,128]{2,1,0:T(8,128)(2,1)S(1)} async-done(((bf16[64,48,128]{2,1,0:T(8,128)(2,1)}), bf16[64,48,128]{2,1,0:T(8,128)(2,1)S(1)}, u32[]{:S(2)}, u32[]{:S(2)}) %all-to-all-start.1) | async-done | bytes 786464 | tf_op jit(solution)/shard_map/all_to_all | solution.py:533
  100.0 9.6 %all_gather.4.notes_ref = bf16[4,104,128]{2,1,0:T(8,128)(2,1)} all-gather(bf16[1,104,128]{2,1,0:T(8,128)(2,1)S(1)} %pad_maximum_fusion.5), channel_id=1, replica_groups=mesh['yh'=2,'core'=2,'yl'=2,'z'=8,'x'=4] {'yh','core'}, dimensions={0}, use_global_device_ids=true | all-gather | bytes 133120 | tf_op jit(solution)/shard_map/all_gather | solution.py:557
  109.6 2.1 %finish.1 = (f32[9,192]{1,0:T(8,128)}, f32[3,192]{1,0:T(4,128)}, f32[12,192]{1,0:T(8,128)}, f32[3,768]{1,0:T(4,128)}, f32[2,3]{1,0:T(2,128)}, /*index=5*/f32[6,16,324]{2,1,0:T(8,128)}) custom-call(s32[4,4]{1,0:T(4,128)} %types_ref.3, bf16[4,104,128]{2,1,0:T(8,128)(2,1)} %all_gather.4.notes_ref), custom_call_target="tpu_custom_call" | custom-call | tf_op jit(solution)/shard_map/finish/pallas_call | solution.py:462
  (65 shorter events, 4.3 us)
Async XLA Ops:
  0.6 45.6 %copy-start = (s32[8,6]{1,0:T(8,128)S(1)}, s32[8,6]{1,0:T(8,128)}, u32[]{:S(2)}) copy-start(s32[8,6]{1,0:T(8,128)} %param.19) | copy-start | bytes 580
  1.8 7.2 %collective-permute-start = (bf16[8,3,12,192]{3,0,2,1:T(8,128)(2,1)S(1)}, bf16[8,3,12,192]{3,0,2,1:T(8,128)(2,1)S(1)}, u32[]{:S(2)}, u32[]{:S(2)}) collective-permute-start(bf16[8,3,12,192]{3,0,2,1:T(8,128)(2,1)S(1)} %get-tuple-element.57), channel_id=1, source_target_pairs={{64,0},{128,64},{192,128},{0,192},{65,1},{129,65},{193,129},{1,193... | collective-permute-start | bytes 331784 | tf_op jit(solution)/shard_map/ppermute | solution.py:27
  5.1 6.1 %collective-permute-start.1 = (bf16[8,3,12,192]{3,0,2,1:T(8,128)(2,1)S(1)}, bf16[8,3,12,192]{3,0,2,1:T(8,128)(2,1)S(1)}, u32[]{:S(2)}, u32[]{:S(2)}) collective-permute-start(bf16[8,3,12,192]{3,0,2,1:T(8,128)(2,1)S(1)} %get-tuple-element.52), channel_id=1, source_target_pairs={{64,0},{128,64},{192,128},{0,192},{65,1},{129,65},{193,129},{1,193... | collective-permute-start | bytes 331784 | tf_op jit(solution)/shard_map/ppermute | solution.py:27
  11.2 35.0 %all-to-all-start = ((bf16[64,48,128]{2,1,0:T(8,128)(2,1)}), bf16[64,48,128]{2,1,0:T(8,128)(2,1)S(1)}, u32[]{:S(2)}, u32[]{:S(2)}) async-start(bf16[64,48,128]{2,1,0:T(8,128)(2,1)} %pack.1), calls=%async_computation | async-start | bytes 1572864 | tf_op jit(solution)/shard_map/all_to_all | solution.py:513
  24.2 7.5 %collective-permute-start.2 = (bf16[144,384]{1,0:T(8,128)(2,1)S(1)}, bf16[144,384]{1,0:T(8,128)(2,1)S(1)}, u32[]{:S(2)}, u32[]{:S(2)}) collective-permute-start(bf16[144,384]{1,0:T(8,128)(2,1)S(1)} %get-tuple-element.45), channel_id=1, source_target_pairs={{3,0},{0,1},{1,2},{2,3},{7,4},{4,5},{5,6},{6,7},{11,8},{8,9},{9,10... | collective-permute-start | bytes 331784 | tf_op jit(solution)/shard_map/ppermute | solution.py:27
  25.3 11.9 %collective-permute-start.3 = (bf16[144,384]{1,0:T(8,128)(2,1)S(1)}, bf16[144,384]{1,0:T(8,128)(2,1)S(1)}, u32[]{:S(2)}, u32[]{:S(2)}) collective-permute-start(bf16[144,384]{1,0:T(8,128)(2,1)S(1)} %get-tuple-element.44), channel_id=1, source_target_pairs={{2,0},{3,1},{0,2},{1,3},{6,4},{7,5},{4,6},{5,7},{10,8},{11,9},{8,1... | collective-permute-start | bytes 331784 | tf_op jit(solution)/shard_map/ppermute | solution.py:27
  27.7 9.5 %collective-permute-start.4 = (bf16[144,384]{1,0:T(8,128)(2,1)S(1)}, bf16[144,384]{1,0:T(8,128)(2,1)S(1)}, u32[]{:S(2)}, u32[]{:S(2)}) collective-permute-start(bf16[144,384]{1,0:T(8,128)(2,1)S(1)} %get-tuple-element.43), channel_id=1, source_target_pairs={{1,0},{2,1},{3,2},{0,3},{5,4},{6,5},{7,6},{4,7},{9,8},{10,9},{11,1... | collective-permute-start | bytes 331784 | tf_op jit(solution)/shard_map/ppermute | solution.py:27
  37.2 6.9 %collective-permute-start.5 = (bf16[144,384]{1,0:T(8,128)(2,1)S(1)}, bf16[144,384]{1,0:T(8,128)(2,1)S(1)}, u32[]{:S(2)}, u32[]{:S(2)}) collective-permute-start(bf16[144,384]{1,0:T(8,128)(2,1)S(1)} %select_select_fusion), channel_id=1, source_target_pairs={{4,0},{8,4},{12,8},{16,12},{20,16},{24,20},{28,24},{32,28},{36,32}... | collective-permute-start | bytes 331784 | tf_op jit(solution)/shard_map/ppermute | solution.py:27
  46.2 2.3 %collective-permute-start.6 = (bf16[64,48,128]{2,1,0:T(8,128)(2,1)S(1)}, bf16[64,48,128]{2,1,0:T(8,128)(2,1)S(1)}, u32[]{:S(2)}, u32[]{:S(2)}) collective-permute-start(bf16[64,48,128]{2,1,0:T(8,128)(2,1)S(1)} %all-to-all-done.landed_ref), channel_id=1, source_target_pairs={{64,0},{0,64},{65,1},{1,65},{66,2},{2,66},{67,3},{3,67},{68,4},{4,... | collective-permute-start | bytes 2359304 | tf_op jit(solution)/shard_map/ppermute | solution.py:27
  65.9 2.0 %collective-permute-start.7 = (bf16[64,27,128]{2,1,0:T(8,128)(2,1)S(1)}, bf16[64,27,128]{2,1,0:T(8,128)(2,1)S(1)}, u32[]{:S(2)}, u32[]{:S(2)}) collective-permute-start(bf16[64,27,128]{2,1,0:T(8,128)(2,1)S(1)} %get-tuple-element.32), channel_id=1, source_target_pairs={{64,0},{0,64},{65,1},{1,65},{66,2},{2,66},{67,3},{3,67},{68,4},{4,... | collective-permute-start | bytes 1327112 | tf_op jit(solution)/shard_map/ppermute | solution.py:27
  69.2 8.2 %collective-permute-start.8 = (bf16[144,192]{1,0:T(8,128)(2,1)S(1)}, bf16[144,192]{1,0:T(8,128)(2,1)S(1)}, u32[]{:S(2)}, u32[]{:S(2)}) collective-permute-start(bf16[144,192]{1,0:T(8,128)(2,1)S(1)} %get-tuple-element.35), channel_id=1, source_target_pairs={{60,0},{0,4},{4,8},{8,12},{12,16},{16,20},{20,24},{24,28},{28,32},... | collective-permute-start | bytes 165896 | tf_op jit(solution)/shard_map/ppermute | solution.py:27
  70.6 28.2 %all-to-all-start.1 = ((bf16[64,48,128]{2,1,0:T(8,128)(2,1)}), bf16[64,48,128]{2,1,0:T(8,128)(2,1)S(1)}, u32[]{:S(2)}, u32[]{:S(2)}) async-start(bf16[64,48,128]{2,1,0:T(8,128)(2,1)} %pad_maximum_fusion), calls=%async_computation.1 | async-start | bytes 1572864 | tf_op jit(solution)/shard_map/all_to_all | solution.py:533
  77.5 3.9 %collective-permute-start.9 = (bf16[144,192]{1,0:T(8,128)(2,1)S(1)}, bf16[144,192]{1,0:T(8,128)(2,1)S(1)}, u32[]{:S(2)}, u32[]{:S(2)}) collective-permute-start(bf16[144,192]{1,0:T(8,128)(2,1)S(1)} %get-tuple-element.49), channel_id=1, source_target_pairs={{1,0},{2,1},{3,2},{0,3},{5,4},{6,5},{7,6},{4,7},{9,8},{10,9},{11,1... | collective-permute-start | bytes 165896 | tf_op jit(solution)/shard_map/ppermute | solution.py:27
  79.8 5.7 %collective-permute-start.10 = (bf16[144,192]{1,0:T(8,128)(2,1)S(1)}, bf16[144,192]{1,0:T(8,128)(2,1)S(1)}, u32[]{:S(2)}, u32[]{:S(2)}) collective-permute-start(bf16[144,192]{1,0:T(8,128)(2,1)S(1)} %get-tuple-element.48), channel_id=1, source_target_pairs={{2,0},{3,1},{0,2},{1,3},{6,4},{7,5},{4,6},{5,7},{10,8},{11,9},{8,1... | collective-permute-start | bytes 165896 | tf_op jit(solution)/shard_map/ppermute | solution.py:27
  80.3 8.3 %collective-permute-start.11 = (bf16[144,192]{1,0:T(8,128)(2,1)S(1)}, bf16[144,192]{1,0:T(8,128)(2,1)S(1)}, u32[]{:S(2)}, u32[]{:S(2)}) collective-permute-start(bf16[144,192]{1,0:T(8,128)(2,1)S(1)} %get-tuple-element.47), channel_id=1, source_target_pairs={{3,0},{0,1},{1,2},{2,3},{7,4},{4,5},{5,6},{6,7},{11,8},{8,9},{9,10... | collective-permute-start | bytes 165896 | tf_op jit(solution)/shard_map/ppermute | solution.py:27
  88.8 6.3 %collective-permute-start.12 = (bf16[4,72,192]{2,1,0:T(8,128)(2,1)S(1)}, bf16[4,72,192]{2,1,0:T(8,128)(2,1)S(1)}, u32[]{:S(2)}, u32[]{:S(2)}) collective-permute-start(bf16[4,72,192]{2,1,0:T(8,128)(2,1)S(1)} %get-tuple-element.50), channel_id=1, source_target_pairs={{192,0},{0,64},{64,128},{128,192},{193,1},{1,65},{65,129},{129,193... | collective-permute-start | bytes 331784 | tf_op jit(solution)/shard_map/ppermute | solution.py:27

commit v4 on v3

--- a/solution.py
+++ b/solution.py
@@ -367,9 +367,9 @@
 
 
 def pack_kernel(
-    spot_ref, types_ref, qkv_ref, proj_ref, up_ref, down_ref, gains_ref, table_ref, out_ref
+    types_ref, qkv_ref, proj_ref, up_ref, down_ref, gains_ref, table_ref, out_ref
 ):
-    x_index, core, lat = spot_ref[0], spot_ref[1], spot_ref[2]
+    x_index, core, lat = lax.axis_index("x"), lax.axis_index("core"), lax.axis_index(LAT)
 
     first = up_ref[...].astype(F32)
     second = jnp.concatenate([qkv_ref[...].astype(F32), proj_ref[...].astype(F32)], axis=0)
@@ -497,11 +497,10 @@
 
     rows = WLAT // 2
     arrived = [passed_along(a[:, :rows], LAT, -1) for a in (inputs, cotangent)]
-    spot = jnp.stack([x_index, core, lat_index]).astype(jnp.int32)
     weights = [w.T for w in (qkv_weight, proj_weight, up_weight, down_weight)]
     weights += [norm_gains, bias_table.transpose(1, 0, 2)]
     (parcel,) = small_call(
-        pack_kernel, (spot, type_of, *weights), 2, [((lons, 48, 128), BF16)], [], "pack"
+        pack_kernel, (type_of, *weights), 1, [((lons, 48, 128), BF16)], [], "pack"
     )
 
     parcel, arrived = lax.optimization_barrier((parcel, arrived))

time: 112 us -> 112 us (level)
  transfers between devices with their start and end apart: 15 -> 15, of which waited for: 12 -> 13; matrix products, arithmetic and copies ran while one was open for 4% -> 3% of each run, Pallas kernels for 2% -> 2%
where the time goes in v4:
time: 112 us
  starting transfers between devices  40.2 us (36%)
  waiting for transfers between devices  32.2 us (29%)
  Pallas kernels  21.9 us (20%)
  blocking collectives  9.59 us (9%)
  other arithmetic  3.6 us (3%)
  local copies, waits for them, and re-layouts  3.21 us (3%)
    ppermute x13, waiting for transfers between devices, passed_along(): lax.ppermute(block, axes, [((i - distance) % size, i) for i in range(size)])  28.1 us
    ppermute x13, starting transfers between devices, passed_along(): lax.ppermute(block, axes, [((i - distance) % size, i) for i in range(size)])  21.6 us
    pallas_call x1, Pallas kernels, block_grads(): pl.pallas_call(block_kernel, in_specs=[pl.BlockSpec(memory_space=pltpu.SM...  17.4 us
    all_to_all x1, starting transfers between devices, shards(): landed = lax.all_to_all(parcel, LON, 0, 0)  11.8 us
    all_gather x1, blocking collectives, shards(): notes = lax.all_gather(note, LAT, axis=0)  9.59 us
    all_to_all x1, starting transfers between devices, shards(): returned = lax.all_to_all(parcel, LON, 0, 0)  6.79 us
    pallas_call x2, Pallas kernels, small_call(): pl.pallas_call(kernel, in_specs=[flat] * scalars + [whole] * (len(args) -...  4.45 us
  transfers between devices with their start and end apart: 15, of which 13 were waited for; matrix products, arithmetic and copies ran while one was open for 3% of the time, Pallas kernels for 2%

profile of v4, /device:TPU:1, one launch (start us, length us, event | category | flops | bytes accessed | tf_op | source)
XLA Modules:
  0.0 111.7 jit_solution(8560747411823548428)
XLA Ops:
  0.6 1.2 %fusion.4 = (bf16[8,3,12,192]{3,0,2,1:T(8,128)(2,1)S(1)}, bf16[8,3,12,192]{3,0,2,1:T(8,128)(2,1)S(1)}, bf16[8,3,12,192]{3,0,2,1:T(8,128)(2,1)S(1)}, bf16[8,3,12,192]{3,0,2,1:T(8,128)(2,1)S(1)}) fusion(bf16[8,6,12,192]{3,0,2,1:T(8,128)(2,1)} %param.11, bf16[8,6,12,192]{3,0,2,1:T(8,128)(2,1)} %param.10), kind=kLoop, calls=%fused_computation.44 | loop fusion | bytes 884736 | tf_op jit(solution)/shard_map/slice | solution.py:499
  1.8 3.3 %collective-permute-start = (bf16[8,3,12,192]{3,0,2,1:T(8,128)(2,1)S(1)}, bf16[8,3,12,192]{3,0,2,1:T(8,128)(2,1)S(1)}, u32[]{:S(2)}, u32[]{:S(2)}) collective-permute-start(bf16[8,3,12,192]{3,0,2,1:T(8,128)(2,1)S(1)} %get-tuple-element.57), channel_id=1, source_target_pairs={{64,0},{128,64},{192,128},{0,192},{65,1},{129,65},{193,129},{1,193... | collective-permute-start | bytes 331784 | tf_op jit(solution)/shard_map/ppermute | solution.py:27
  5.1 0.9 collective-permute-start.1
  6.0 2.4 %pack.1 = bf16[64,48,128]{2,1,0:T(8,128)(2,1)} custom-call(s32[4,4]{1,0:T(4,128)} %types_ref.3, bf16[9,192]{1,0:T(8,128)(2,1)} %bitcast.86, bf16[3,192]{1,0:T(4,128)(2,1)} %bitcast.89, bf16[12,192]{1,0:T(8,128)(2,1)} %bitcast.87, bf16[3,768]{1,0:T(4,128)(2,1)} %bitcast.88, bf16[2,3]{1,0:T(2,128)(2,1)} %gains_ref.1, bf16[6,16,324]{2,1,0:T(8,128)(2,1)} %bitcast.81), custom_call_target="tpu_custom_call" | custom-call | tf_op jit(solution)/shard_map/pack/pallas_call | solution.py:462
  8.4 0.6 collective-permute-done
  9.0 2.2 %collective-permute-done.1 = bf16[8,3,12,192]{3,0,2,1:T(8,128)(2,1)S(1)} collective-permute-done((bf16[8,3,12,192]{3,0,2,1:T(8,128)(2,1)S(1)}, bf16[8,3,12,192]{3,0,2,1:T(8,128)(2,1)S(1)}, u32[]{:S(2)}, u32[]{:S(2)}) %collective-permute-start.1) | collective-permute-done | bytes 110624 | tf_op jit(solution)/shard_map/ppermute | solution.py:27
  11.2 11.8 %all-to-all-start = ((bf16[64,48,128]{2,1,0:T(8,128)(2,1)}), bf16[64,48,128]{2,1,0:T(8,128)(2,1)S(1)}, u32[]{:S(2)}, u32[]{:S(2)}) async-start(bf16[64,48,128]{2,1,0:T(8,128)(2,1)} %pack.1), calls=%async_computation | async-start | bytes 1572864 | tf_op jit(solution)/shard_map/all_to_all | solution.py:512
  24.2 1.1 collective-permute-start.2
  25.3 2.4 %collective-permute-start.3 = (bf16[144,384]{1,0:T(8,128)(2,1)S(1)}, bf16[144,384]{1,0:T(8,128)(2,1)S(1)}, u32[]{:S(2)}, u32[]{:S(2)}) collective-permute-start(bf16[144,384]{1,0:T(8,128)(2,1)S(1)} %get-tuple-element.44), channel_id=1, source_target_pairs={{2,0},{3,1},{0,2},{1,3},{6,4},{7,5},{4,6},{5,7},{10,8},{11,9},{8,1... | collective-permute-start | bytes 331784 | tf_op jit(solution)/shard_map/ppermute | solution.py:27
  27.7 1.2 %collective-permute-start.4 = (bf16[144,384]{1,0:T(8,128)(2,1)S(1)}, bf16[144,384]{1,0:T(8,128)(2,1)S(1)}, u32[]{:S(2)}, u32[]{:S(2)}) collective-permute-start(bf16[144,384]{1,0:T(8,128)(2,1)S(1)} %get-tuple-element.43), channel_id=1, source_target_pairs={{1,0},{2,1},{3,2},{0,3},{5,4},{6,5},{7,6},{4,7},{9,8},{10,9},{11,1... | collective-permute-start | bytes 331784 | tf_op jit(solution)/shard_map/ppermute | solution.py:27
  28.9 2.8 %collective-permute-done.2.b1 = bf16[144,384]{1,0:T(8,128)(2,1)S(1)} collective-permute-done((bf16[144,384]{1,0:T(8,128)(2,1)S(1)}, bf16[144,384]{1,0:T(8,128)(2,1)S(1)}, u32[]{:S(2)}, u32[]{:S(2)}) %collective-permute-start.2) | collective-permute-done | bytes 110624 | tf_op jit(solution)/shard_map/ppermute | solution.py:27
  31.7 5.5 %collective-permute-done.3.b2 = bf16[144,384]{1,0:T(8,128)(2,1)S(1)} collective-permute-done((bf16[144,384]{1,0:T(8,128)(2,1)S(1)}, bf16[144,384]{1,0:T(8,128)(2,1)S(1)}, u32[]{:S(2)}, u32[]{:S(2)}) %collective-permute-start.3) | collective-permute-done | bytes 110624 | tf_op jit(solution)/shard_map/ppermute | solution.py:27
  37.2 4.8 %collective-permute-start.5 = (bf16[144,384]{1,0:T(8,128)(2,1)S(1)}, bf16[144,384]{1,0:T(8,128)(2,1)S(1)}, u32[]{:S(2)}, u32[]{:S(2)}) collective-permute-start(bf16[144,384]{1,0:T(8,128)(2,1)S(1)} %select_select_fusion), channel_id=1, source_target_pairs={{4,0},{8,4},{12,8},{16,12},{20,16},{24,20},{28,24},{32,28},{36,32}... | collective-permute-start | bytes 331784 | tf_op jit(solution)/shard_map/ppermute | solution.py:27
  42.1 2.1 %collective-permute-done.5.rim_ref = bf16[144,384]{1,0:T(8,128)(2,1)S(1)} collective-permute-done((bf16[144,384]{1,0:T(8,128)(2,1)S(1)}, bf16[144,384]{1,0:T(8,128)(2,1)S(1)}, u32[]{:S(2)}, u32[]{:S(2)}) %collective-permute-start.5) | collective-permute-done | bytes 110624 | tf_op jit(solution)/shard_map/ppermute | solution.py:27
  44.2 2.1 %all-to-all-done.landed_ref = bf16[64,48,128]{2,1,0:T(8,128)(2,1)S(1)} async-done(((bf16[64,48,128]{2,1,0:T(8,128)(2,1)}), bf16[64,48,128]{2,1,0:T(8,128)(2,1)S(1)}, u32[]{:S(2)}, u32[]{:S(2)}) %all-to-all-start) | async-done | bytes 786464 | tf_op jit(solution)/shard_map/all_to_all | solution.py:512
  46.5 2.0 %collective-permute-done.6.halves_ref = bf16[64,48,128]{2,1,0:T(8,128)(2,1)S(1)} collective-permute-done((bf16[64,48,128]{2,1,0:T(8,128)(2,1)S(1)}, bf16[64,48,128]{2,1,0:T(8,128)(2,1)S(1)}, u32[]{:S(2)}, u32[]{:S(2)}) %collective-permute-start.6) | collective-permute-done | bytes 786464 | tf_op jit(solution)/shard_map/ppermute | solution.py:27
  48.5 17.4 %block_grads.1 = (bf16[4,144,192]{2,1,0:T(8,128)(2,1)S(1)}, bf16[144,192]{1,0:T(8,128)(2,1)S(1)}, bf16[64,27,128]{2,1,0:T(8,128)(2,1)S(1)}, bf16[64,27,128]{2,1,0:T(8,128)(2,1)S(1)}, bf16[64,21,128]{2,1,0:T(8,128)(2,1)S(1)}) custom-call(s32[1]{0:T(128)} %bitcast.last_ref, s32[1]{0:T(128)} %bitcast.1.core_ref, bf16[144,384]{1,0:T(8,128)(2,1)S(1)} %get-tuple-element.46.b0, ...), custom_call_target="tpu_custom_call" | custom-call | tf_op jit(solution)/shard_map/block_grads/pallas_call | solution.py:350
  66.2 1.8 %collective-permute-done.7 = bf16[64,27,128]{2,1,0:T(8,128)(2,1)S(1)} collective-permute-done((bf16[64,27,128]{2,1,0:T(8,128)(2,1)S(1)}, bf16[64,27,128]{2,1,0:T(8,128)(2,1)S(1)}, u32[]{:S(2)}, u32[]{:S(2)}) %collective-permute-start.7) | collective-permute-done | bytes 442400 | tf_op jit(solution)/shard_map/ppermute | solution.py:27
  68.1 1.1 pad_maximum_fusion
  69.2 1.4 %collective-permute-start.8 = (bf16[144,192]{1,0:T(8,128)(2,1)S(1)}, bf16[144,192]{1,0:T(8,128)(2,1)S(1)}, u32[]{:S(2)}, u32[]{:S(2)}) collective-permute-start(bf16[144,192]{1,0:T(8,128)(2,1)S(1)} %get-tuple-element.35), channel_id=1, source_target_pairs={{60,0},{0,4},{4,8},{8,12},{12,16},{16,20},{20,24},{24,28},{28,32},... | collective-permute-start | bytes 165896 | tf_op jit(solution)/shard_map/ppermute | solution.py:27
  70.6 6.8 %all-to-all-start.1 = ((bf16[64,48,128]{2,1,0:T(8,128)(2,1)}), bf16[64,48,128]{2,1,0:T(8,128)(2,1)S(1)}, u32[]{:S(2)}, u32[]{:S(2)}) async-start(bf16[64,48,128]{2,1,0:T(8,128)(2,1)} %pad_maximum_fusion), calls=%async_computation.1 | async-start | bytes 1572864 | tf_op jit(solution)/shard_map/all_to_all | solution.py:532
  77.5 2.3 %collective-permute-start.9 = (bf16[144,192]{1,0:T(8,128)(2,1)S(1)}, bf16[144,192]{1,0:T(8,128)(2,1)S(1)}, u32[]{:S(2)}, u32[]{:S(2)}) collective-permute-start(bf16[144,192]{1,0:T(8,128)(2,1)S(1)} %get-tuple-element.49), channel_id=1, source_target_pairs={{1,0},{2,1},{3,2},{0,3},{5,4},{6,5},{7,6},{4,7},{9,8},{10,9},{11,1... | collective-permute-start | bytes 165896 | tf_op jit(solution)/shard_map/ppermute | solution.py:27
  79.8 0.6 collective-permute-start.10
  80.4 0.6 collective-permute-start.11
  81.4 4.0 %collective-permute-done.10 = bf16[144,192]{1,0:T(8,128)(2,1)S(1)} collective-permute-done((bf16[144,192]{1,0:T(8,128)(2,1)S(1)}, bf16[144,192]{1,0:T(8,128)(2,1)S(1)}, u32[]{:S(2)}, u32[]{:S(2)}) %collective-permute-start.10) | collective-permute-done | bytes 55328 | tf_op jit(solution)/shard_map/ppermute | solution.py:27
  85.4 3.2 %collective-permute-done.11 = bf16[144,192]{1,0:T(8,128)(2,1)S(1)} collective-permute-done((bf16[144,192]{1,0:T(8,128)(2,1)S(1)}, bf16[144,192]{1,0:T(8,128)(2,1)S(1)}, u32[]{:S(2)}, u32[]{:S(2)}) %collective-permute-start.11) | collective-permute-done | bytes 55328 | tf_op jit(solution)/shard_map/ppermute | solution.py:27
  88.8 2.8 %collective-permute-start.12 = (bf16[4,72,192]{2,1,0:T(8,128)(2,1)S(1)}, bf16[4,72,192]{2,1,0:T(8,128)(2,1)S(1)}, u32[]{:S(2)}, u32[]{:S(2)}) collective-permute-start(bf16[4,72,192]{2,1,0:T(8,128)(2,1)S(1)} %get-tuple-element.50), channel_id=1, source_target_pairs={{192,0},{0,64},{64,128},{128,192},{193,1},{1,65},{65,129},{129,193... | collective-permute-start | bytes 331784 | tf_op jit(solution)/shard_map/ppermute | solution.py:27
  91.6 3.5 %collective-permute-done.12 = bf16[4,72,192]{2,1,0:T(8,128)(2,1)S(1)} collective-permute-done((bf16[4,72,192]{2,1,0:T(8,128)(2,1)S(1)}, bf16[4,72,192]{2,1,0:T(8,128)(2,1)S(1)}, u32[]{:S(2)}, u32[]{:S(2)}) %collective-permute-start.12) | collective-permute-done | bytes 110624 | tf_op jit(solution)/shard_map/ppermute | solution.py:27
  96.0 0.9 pad_maximum_fusion.1
  96.9 2.0 %all-to-all-done.1 = bf16[64,48,128]{2,1,0:T(8,128)(2,1)S(1)} async-done(((bf16[64,48,128]{2,1,0:T(8,128)(2,1)}), bf16[64,48,128]{2,1,0:T(8,128)(2,1)S(1)}, u32[]{:S(2)}, u32[]{:S(2)}) %all-to-all-start.1) | async-done | bytes 786464 | tf_op jit(solution)/shard_map/all_to_all | solution.py:532
  100.0 9.6 %all_gather.4.notes_ref = bf16[4,104,128]{2,1,0:T(8,128)(2,1)} all-gather(bf16[1,104,128]{2,1,0:T(8,128)(2,1)S(1)} %pad_maximum_fusion.5), channel_id=1, replica_groups=mesh['yh'=2,'core'=2,'yl'=2,'z'=8,'x'=4] {'yh','core'}, dimensions={0}, use_global_device_ids=true | all-gather | bytes 133120 | tf_op jit(solution)/shard_map/all_gather | solution.py:556
  109.6 2.1 %finish.1 = (f32[9,192]{1,0:T(8,128)}, f32[3,192]{1,0:T(4,128)}, f32[12,192]{1,0:T(8,128)}, f32[3,768]{1,0:T(4,128)}, f32[2,3]{1,0:T(2,128)}, /*index=5*/f32[6,16,324]{2,1,0:T(8,128)}) custom-call(s32[4,4]{1,0:T(4,128)} %types_ref.3, bf16[4,104,128]{2,1,0:T(8,128)(2,1)} %all_gather.4.notes_ref), custom_call_target="tpu_custom_call" | custom-call | tf_op jit(solution)/shard_map/finish/pallas_call | solution.py:462
  (64 shorter events, 4.3 us)
Async XLA Ops:
  0.6 45.6 %copy-start = (s32[8,6]{1,0:T(8,128)S(1)}, s32[8,6]{1,0:T(8,128)}, u32[]{:S(2)}) copy-start(s32[8,6]{1,0:T(8,128)} %param.19) | copy-start | bytes 580
  1.8 7.2 %collective-permute-start = (bf16[8,3,12,192]{3,0,2,1:T(8,128)(2,1)S(1)}, bf16[8,3,12,192]{3,0,2,1:T(8,128)(2,1)S(1)}, u32[]{:S(2)}, u32[]{:S(2)}) collective-permute-start(bf16[8,3,12,192]{3,0,2,1:T(8,128)(2,1)S(1)} %get-tuple-element.57), channel_id=1, source_target_pairs={{64,0},{128,64},{192,128},{0,192},{65,1},{129,65},{193,129},{1,193... | collective-permute-start | bytes 331784 | tf_op jit(solution)/shard_map/ppermute | solution.py:27
  5.1 6.1 %collective-permute-start.1 = (bf16[8,3,12,192]{3,0,2,1:T(8,128)(2,1)S(1)}, bf16[8,3,12,192]{3,0,2,1:T(8,128)(2,1)S(1)}, u32[]{:S(2)}, u32[]{:S(2)}) collective-permute-start(bf16[8,3,12,192]{3,0,2,1:T(8,128)(2,1)S(1)} %get-tuple-element.52), channel_id=1, source_target_pairs={{64,0},{128,64},{192,128},{0,192},{65,1},{129,65},{193,129},{1,193... | collective-permute-start | bytes 331784 | tf_op jit(solution)/shard_map/ppermute | solution.py:27
  11.2 35.0 %all-to-all-start = ((bf16[64,48,128]{2,1,0:T(8,128)(2,1)}), bf16[64,48,128]{2,1,0:T(8,128)(2,1)S(1)}, u32[]{:S(2)}, u32[]{:S(2)}) async-start(bf16[64,48,128]{2,1,0:T(8,128)(2,1)} %pack.1), calls=%async_computation | async-start | bytes 1572864 | tf_op jit(solution)/shard_map/all_to_all | solution.py:512
  24.2 7.5 %collective-permute-start.2 = (bf16[144,384]{1,0:T(8,128)(2,1)S(1)}, bf16[144,384]{1,0:T(8,128)(2,1)S(1)}, u32[]{:S(2)}, u32[]{:S(2)}) collective-permute-start(bf16[144,384]{1,0:T(8,128)(2,1)S(1)} %get-tuple-element.45), channel_id=1, source_target_pairs={{3,0},{0,1},{1,2},{2,3},{7,4},{4,5},{5,6},{6,7},{11,8},{8,9},{9,10... | collective-permute-start | bytes 331784 | tf_op jit(solution)/shard_map/ppermute | solution.py:27
  25.3 11.9 %collective-permute-start.3 = (bf16[144,384]{1,0:T(8,128)(2,1)S(1)}, bf16[144,384]{1,0:T(8,128)(2,1)S(1)}, u32[]{:S(2)}, u32[]{:S(2)}) collective-permute-start(bf16[144,384]{1,0:T(8,128)(2,1)S(1)} %get-tuple-element.44), channel_id=1, source_target_pairs={{2,0},{3,1},{0,2},{1,3},{6,4},{7,5},{4,6},{5,7},{10,8},{11,9},{8,1... | collective-permute-start | bytes 331784 | tf_op jit(solution)/shard_map/ppermute | solution.py:27
  27.7 9.5 %collective-permute-start.4 = (bf16[144,384]{1,0:T(8,128)(2,1)S(1)}, bf16[144,384]{1,0:T(8,128)(2,1)S(1)}, u32[]{:S(2)}, u32[]{:S(2)}) collective-permute-start(bf16[144,384]{1,0:T(8,128)(2,1)S(1)} %get-tuple-element.43), channel_id=1, source_target_pairs={{1,0},{2,1},{3,2},{0,3},{5,4},{6,5},{7,6},{4,7},{9,8},{10,9},{11,1... | collective-permute-start | bytes 331784 | tf_op jit(solution)/shard_map/ppermute | solution.py:27
  37.2 6.9 %collective-permute-start.5 = (bf16[144,384]{1,0:T(8,128)(2,1)S(1)}, bf16[144,384]{1,0:T(8,128)(2,1)S(1)}, u32[]{:S(2)}, u32[]{:S(2)}) collective-permute-start(bf16[144,384]{1,0:T(8,128)(2,1)S(1)} %select_select_fusion), channel_id=1, source_target_pairs={{4,0},{8,4},{12,8},{16,12},{20,16},{24,20},{28,24},{32,28},{36,32}... | collective-permute-start | bytes 331784 | tf_op jit(solution)/shard_map/ppermute | solution.py:27
  46.2 2.3 %collective-permute-start.6 = (bf16[64,48,128]{2,1,0:T(8,128)(2,1)S(1)}, bf16[64,48,128]{2,1,0:T(8,128)(2,1)S(1)}, u32[]{:S(2)}, u32[]{:S(2)}) collective-permute-start(bf16[64,48,128]{2,1,0:T(8,128)(2,1)S(1)} %all-to-all-done.landed_ref), channel_id=1, source_target_pairs={{64,0},{0,64},{65,1},{1,65},{66,2},{2,66},{67,3},{3,67},{68,4},{4,... | collective-permute-start | bytes 2359304 | tf_op jit(solution)/shard_map/ppermute | solution.py:27
  66.0 2.0 %collective-permute-start.7 = (bf16[64,27,128]{2,1,0:T(8,128)(2,1)S(1)}, bf16[64,27,128]{2,1,0:T(8,128)(2,1)S(1)}, u32[]{:S(2)}, u32[]{:S(2)}) collective-permute-start(bf16[64,27,128]{2,1,0:T(8,128)(2,1)S(1)} %get-tuple-element.32), channel_id=1, source_target_pairs={{64,0},{0,64},{65,1},{1,65},{66,2},{2,66},{67,3},{3,67},{68,4},{4,... | collective-permute-start | bytes 1327112 | tf_op jit(solution)/shard_map/ppermute | solution.py:27
  69.2 8.2 %collective-permute-start.8 = (bf16[144,192]{1,0:T(8,128)(2,1)S(1)}, bf16[144,192]{1,0:T(8,128)(2,1)S(1)}, u32[]{:S(2)}, u32[]{:S(2)}) collective-permute-start(bf16[144,192]{1,0:T(8,128)(2,1)S(1)} %get-tuple-element.35), channel_id=1, source_target_pairs={{60,0},{0,4},{4,8},{8,12},{12,16},{16,20},{20,24},{24,28},{28,32},... | collective-permute-start | bytes 165896 | tf_op jit(solution)/shard_map/ppermute | solution.py:27
  70.6 28.2 %all-to-all-start.1 = ((bf16[64,48,128]{2,1,0:T(8,128)(2,1)}), bf16[64,48,128]{2,1,0:T(8,128)(2,1)S(1)}, u32[]{:S(2)}, u32[]{:S(2)}) async-start(bf16[64,48,128]{2,1,0:T(8,128)(2,1)} %pad_maximum_fusion), calls=%async_computation.1 | async-start | bytes 1572864 | tf_op jit(solution)/shard_map/all_to_all | solution.py:532
  77.5 3.9 %collective-permute-start.9 = (bf16[144,192]{1,0:T(8,128)(2,1)S(1)}, bf16[144,192]{1,0:T(8,128)(2,1)S(1)}, u32[]{:S(2)}, u32[]{:S(2)}) collective-permute-start(bf16[144,192]{1,0:T(8,128)(2,1)S(1)} %get-tuple-element.49), channel_id=1, source_target_pairs={{1,0},{2,1},{3,2},{0,3},{5,4},{6,5},{7,6},{4,7},{9,8},{10,9},{11,1... | collective-permute-start | bytes 165896 | tf_op jit(solution)/shard_map/ppermute | solution.py:27
  79.8 5.7 %collective-permute-start.10 = (bf16[144,192]{1,0:T(8,128)(2,1)S(1)}, bf16[144,192]{1,0:T(8,128)(2,1)S(1)}, u32[]{:S(2)}, u32[]{:S(2)}) collective-permute-start(bf16[144,192]{1,0:T(8,128)(2,1)S(1)} %get-tuple-element.48), channel_id=1, source_target_pairs={{2,0},{3,1},{0,2},{1,3},{6,4},{7,5},{4,6},{5,7},{10,8},{11,9},{8,1... | collective-permute-start | bytes 165896 | tf_op jit(solution)/shard_map/ppermute | solution.py:27
  80.4 8.3 %collective-permute-start.11 = (bf16[144,192]{1,0:T(8,128)(2,1)S(1)}, bf16[144,192]{1,0:T(8,128)(2,1)S(1)}, u32[]{:S(2)}, u32[]{:S(2)}) collective-permute-start(bf16[144,192]{1,0:T(8,128)(2,1)S(1)} %get-tuple-element.47), channel_id=1, source_target_pairs={{3,0},{0,1},{1,2},{2,3},{7,4},{4,5},{5,6},{6,7},{11,8},{8,9},{9,10... | collective-permute-start | bytes 165896 | tf_op jit(solution)/shard_map/ppermute | solution.py:27
  88.8 6.3 %collective-permute-start.12 = (bf16[4,72,192]{2,1,0:T(8,128)(2,1)S(1)}, bf16[4,72,192]{2,1,0:T(8,128)(2,1)S(1)}, u32[]{:S(2)}, u32[]{:S(2)}) collective-permute-start(bf16[4,72,192]{2,1,0:T(8,128)(2,1)S(1)} %get-tuple-element.50), channel_id=1, source_target_pairs={{192,0},{0,64},{64,128},{128,192},{193,1},{1,65},{65,129},{129,193... | collective-permute-start | bytes 331784 | tf_op jit(solution)/shard_map/ppermute | solution.py:27
